TPU v7x, 32 devices: a whole 2x2x4 slice. The times are simulated.
32 devices in a mesh: leaf: 32 (over z, y, x, core).
Axes of the slice: x: 2, y: 2, z: 4, core: 2. Of those that a mesh axis runs over, the one named last changes fastest.
Arguments:
- near_blocks: bfloat16 [64, 26, 256, 256], P('leaf'), may hold values from -0.0582 to 0.0582
- diag_blocks: bfloat16 [64, 256, 256], P('leaf'), as said below
- bases: bfloat16 [64, 256, 256], P('leaf'), as said below
- leaf_nbrs: int32 [64, 26], P('leaf'), may hold values from -1 to 63, as said below
- parent_nbrs: int32 [8, 5], replicated, may hold values from 0 to 7, as said below
Outputs:
- leaf_factor: float32 [64, 128, 128], P('leaf')
- leaf_panel: float32 [64, 128, 128], P('leaf')
- merged: float32 [64, 5, 128, 1024], P('leaf')
- parent_block: float32 [8192, 1024], P('leaf')
Inputs may be any that keep to these rules, and one draw needn't show every extreme that they name: `leaf_nbrs`: row i lists distinct leaves j with j != i and |j - i| <= 16; live entries come first and -1 fills the rest; every row has at least 13 live entries and some row has all 26. `parent_nbrs`: row P begins with P itself, followed by the other 4 parents nearest to P in numbering, distinct, equally near ones in any order. `diag_blocks`: each block is symmetric positive definite. `bases`: each basis is an orthogonal matrix rounded to bfloat16.
All inputs are finite; a program needn't handle non-finite values.
Results may differ from a plain program's by a relative error of at most 0.001.
The roundings to bfloat16 on the way count: a program that leaves them out, or rounds other values in their place, can miss the bound.
Values may be sent and summed in bfloat16 or wider, within the bound.
A program may use at most 128 MiB of HBM per device.

v0:
```python
import functools

import jax
import jax.numpy as jnp
from jax import lax
from jax.experimental import pallas as pl
from jax.experimental.pallas import tpu as pltpu
from jax.sharding import PartitionSpec as P

RANK = 128
REACH = 16
CHILDREN = 8
PANEL = 32
MESH = pl.DeviceIdType.MESH
highest = lax.Precision.HIGHEST


def matmul(a, b):
    return jnp.dot(a, b, preferred_element_type=jnp.float32)


def matmul_t(a, b, precision=None):
    return lax.dot_general(
        a, b, (((0,), (0,)), ((), ())), preferred_element_type=jnp.float32, precision=precision
    )


def eliminate(diag, bases, factor, panel, skeleton, shift, shift_t2, bases_t, work, rows):
    per_device, leaf_rows = bases.shape[0], bases.shape[1]
    red = leaf_rows - RANK
    wide = 2 * red + RANK
    row_id = lax.broadcasted_iota(jnp.int32, (red, red), 0)
    col_id = lax.broadcasted_iota(jnp.int32, (red, red), 1)
    low_corner = []
    for leaf in range(per_device):
        basis = bases[leaf]
        basis_t = basis.T
        bases_t[leaf] = basis_t
        half = matmul(basis_t, diag[leaf]).astype(jnp.bfloat16)
        dense = matmul(half, basis)
        top = dense[:red, :red]
        work[leaf, :, :red] = 0.5 * (top + top.T)
        work[leaf, :, red : red + RANK] = dense[:red, red:]
        work[leaf, :, red + RANK :] = (row_id == col_id).astype(jnp.float32)
        low_corner.append(dense[red:, red:])
    sub = lax.broadcasted_iota(jnp.int32, (PANEL, 1), 0)
    for start in range(0, red, PANEL):
        strips = [work[leaf, start : start + PANEL, :] for leaf in range(per_device)]
        for k in range(PANEL):
            for leaf in range(per_device):
                strip = strips[leaf]
                column = strip[:, start + k : start + k + 1]
                ratio = jnp.where(sub > k, column / column[k : k + 1], 0.0)
                strips[leaf] = strip - ratio * strip[k : k + 1, :]
        lane = lax.broadcasted_iota(jnp.int32, (PANEL, wide), 1)
        line = lax.broadcasted_iota(jnp.int32, (PANEL, wide), 0)
        for leaf in range(per_device):
            strip = strips[leaf]
            pivots = jnp.sum(jnp.where(lane == line + start, strip, 0.0), axis=1, keepdims=True)
            strip = strip * (1.0 / jnp.sqrt(pivots))
            rows[leaf, start : start + PANEL, :] = strip
            if start + PANEL < red:
                work[leaf] = work[leaf] - matmul_t(strip[:, :red], strip, highest)
    for leaf in range(per_device):
        solved = rows[leaf, :, red : red + RANK]
        inverse = jnp.where(col_id <= row_id, rows[leaf, :, red + RANK :], 0.0)
        moved = matmul_t(inverse, solved, highest)
        shift[leaf] = moved.astype(jnp.bfloat16)
        turned = moved.T.astype(jnp.bfloat16)
        shift_t2[leaf, :, :red] = turned
        shift_t2[leaf, :, red:] = turned
    for leaf in range(per_device):
        solved = rows[leaf, :, red : red + RANK]
        panel[leaf] = solved
        skeleton[leaf] = low_corner[leaf] - matmul_t(solved, solved, highest)
        upper = jnp.where(col_id >= row_id, rows[leaf, :, :red], 0.0)
        factor[leaf] = upper.T


def window_kernel(
    chips,
    count,
    diag,
    bases,
    near,
    factor,
    panel,
    skeleton,
    shift_t2,
    halves,
    win_bases,
    win_shift,
    shift,
    bases_t,
    work,
    rows,
    near_in,
    half_out,
    send,
    recv,
    pass_send,
    pass_recv,
    own_sem,
    near_sem,
    half_sem,
):
    per_device, slots = near_in.shape[0], near_in.shape[1]
    fetches = [
        pltpu.make_async_copy(near.at[leaf], near_in.at[leaf], near_sem.at[leaf])
        for leaf in range(per_device)
    ]
    stores = [
        pltpu.make_async_copy(
            half_out.at[leaf], halves.at[leaf, pl.ds(0, slots)], half_sem.at[leaf]
        )
        for leaf in range(per_device)
    ]
    me = lax.axis_index("leaf")
    core = me % 2
    sibling = me + 1 - 2 * core
    offsets = [sign * step for step in range(chips, 0, -1) for sign in (1, -1)]
    pairs = ((bases, win_bases), (shift, win_shift))

    def inside(offset):
        other = me + 2 * offset
        return (other >= 0) & (other < count)

    barrier = pltpu.get_barrier_semaphore()
    pl.semaphore_signal(barrier, inc=1, device_id=(sibling,), device_id_type=MESH)
    for offset in offsets:

        @pl.when(inside(offset))
        def _(offset=offset):
            pl.semaphore_signal(barrier, inc=1, device_id=(me + 2 * offset,), device_id_type=MESH)

    peers = jnp.int32(1)
    for offset in offsets:
        peers = peers + inside(offset).astype(jnp.int32)
    pl.semaphore_wait(barrier, peers)

    def direct(kind, offset):
        source, window = pairs[kind]
        return pltpu.make_async_remote_copy(
            src_ref=source,
            dst_ref=window.at[2 * (chips - offset) + core],
            send_sem=send.at[kind, chips + offset],
            recv_sem=recv.at[kind, chips - offset],
            device_id=(me + 2 * offset,),
            device_id_type=MESH,
        )

    def arrival(kind, offset):
        source, window = pairs[kind]
        return pltpu.make_async_remote_copy(
            src_ref=source,
            dst_ref=window.at[2 * (chips + offset) + core],
            send_sem=send.at[kind, chips + offset],
            recv_sem=recv.at[kind, chips + offset],
            device_id=(sibling,),
            device_id_type=MESH,
        )

    def relay(kind, offset):
        source, window = pairs[kind]
        slot = 2 * (chips + offset) + core
        return pltpu.make_async_remote_copy(
            src_ref=source if offset == 0 else window.at[slot],
            dst_ref=window.at[slot],
            send_sem=pass_send.at[kind, chips + offset],
            recv_sem=pass_recv.at[kind, chips + offset],
            device_id=(sibling,),
            device_id_type=MESH,
        )

    def relayed(kind, offset):
        source, window = pairs[kind]
        slot = 2 * (chips + offset) + 1 - core
        return pltpu.make_async_remote_copy(
            src_ref=source,
            dst_ref=window.at[slot],
            send_sem=pass_send.at[kind, chips + offset],
            recv_sem=pass_recv.at[kind, chips + offset],
            device_id=(sibling,),
            device_id_type=MESH,
        )

    def dispatch(kind):
        for offset in offsets:

            @pl.when(inside(offset))
            def _(offset=offset):
                direct(kind, offset).start()

        relay(kind, 0).start()
        source, window = pairs[kind]
        pltpu.make_async_copy(source, window.at[2 * chips + core], own_sem.at[kind]).start()

    def hand_on(kind, offset):
        @pl.when(inside(offset))
        def _():
            arrival(kind, offset).wait_recv()
            relay(kind, offset).start()

    def project(first, last):
        @pl.loop(first, last)
        def _(n):
            for leaf in range(per_device):
                half_out[leaf, n] = matmul(bases_t[leaf], near_in[leaf, n]).astype(jnp.bfloat16)

    dispatch(0)
    for fetch in fetches:
        fetch.start()
    eliminate(diag, bases, factor, panel, skeleton, shift, shift_t2, bases_t, work, rows)
    dispatch(1)
    for fetch in fetches:
        fetch.wait()
    nearest = offsets[::-1]
    done = 0
    for turn, offset in enumerate(nearest):
        hand_on(0, offset)
        upto = slots * (turn + 1) // len(nearest)
        project(done, upto)
        done = upto
    for store in stores:
        store.start()
    for offset in nearest:
        hand_on(1, offset)

    for kind in range(2):
        source, window = pairs[kind]
        pltpu.make_async_copy(source, window.at[2 * chips + core], own_sem.at[kind]).wait()
        relay(kind, 0).wait_send()
        relayed(kind, 0).wait_recv()
        for offset in offsets:

            @pl.when(inside(offset))
            def _(kind=kind, offset=offset):
                direct(kind, offset).wait_send()
                relay(kind, offset).wait_send()
                relayed(kind, offset).wait_recv()

    for store in stores:
        store.wait()


def couple_kernel(
    chips,
    group,
    slots,
    where,
    nbrs,
    parents,
    halves,
    shift_t2,
    skeleton,
    win_bases,
    win_shift,
    merged,
    diagonal,
):
    leaf, step = pl.program_id(0), pl.program_id(1)
    per_device = pl.num_programs(0)
    steps = pl.num_programs(1)
    red = shift_t2.shape[2] // 2
    me = where[0]
    number = me * per_device + leaf
    parent = number // CHILDREN
    targets = parents.shape[1]

    @pl.when(step == 0)
    def _():
        merged[...] = jnp.zeros_like(merged)
        place = pl.multiple_of((number % CHILDREN) * RANK, RANK)
        for q in range(targets):

            @pl.when(parents[parent, q] == parent)
            def _(q=q):
                merged[0, q, :, pl.ds(place, RANK)] = skeleton[0]

    @pl.when(nbrs[leaf, step * group] >= 0)
    def _():
        results = []
        for k in range(group):
            n = step * group + k
            other = jnp.where(n < slots, nbrs[leaf, jnp.minimum(n, slots - 1)], -1)
            safe = jnp.where(other >= 0, other, number)
            owner = safe // per_device
            slot = (owner // 2 - me // 2 + chips) * 2 + owner % 2
            basis = win_bases[slot, safe % per_device]
            moved = win_shift[slot, safe % per_device]
            half = halves[0, k]
            right = matmul(half, basis[:, red:])
            left = matmul(half[red:], basis[:, :red])
            high = right[:red].astype(jnp.bfloat16)
            low = (right[:red] - high.astype(jnp.float32)).astype(jnp.bfloat16)
            first = matmul(shift_t2[0], jnp.concatenate([high, low], axis=0))
            high = left.astype(jnp.bfloat16)
            low = (left - high.astype(jnp.float32)).astype(jnp.bfloat16)
            second = matmul(
                jnp.concatenate([high, low], axis=1), jnp.concatenate([moved, moved], axis=0)
            )
            q = jnp.int32(-1)
            for place in range(targets):
                q = jnp.where(parents[parent, place] == safe // CHILDREN, place, q)
            results.append((right[red:] - first - second, other, q))
        for schur, other, q in results:

            @pl.when((other >= 0) & (q >= 0))
            def _(schur=schur, other=other, q=q):
                place = pl.multiple_of((other % CHILDREN) * RANK, RANK)
                merged[0, q, :, pl.ds(place, RANK)] = schur

    @pl.when(step == steps - 1)
    def _():
        diagonal[0] = merged[0, 0].astype(jnp.bfloat16)


def parent_kernel(size, own, diagonal, block, landed, send, recv):
    me = lax.axis_index("leaf")
    place = me % size
    base = me - place
    per_device, rank = own.shape[0], own.shape[2]
    width = per_device * rank
    barrier = pltpu.get_barrier_semaphore()
    for t in range(1, size):
        pl.semaphore_signal(
            barrier, inc=1, device_id=(base + (place + t) % size,), device_id_type=MESH
        )
    pl.semaphore_wait(barrier, size - 1)

    def copy(t):
        other = (place + t) % size
        return pltpu.make_async_remote_copy(
            src_ref=diagonal.at[:, :, pl.ds(pl.multiple_of(other * width, 128), width)],
            dst_ref=landed.at[size - t],
            send_sem=send.at[t],
            recv_sem=recv.at[size - t],
            device_id=(base + other,),
            device_id_type=MESH,
        )

    for t in range(1, size):
        copy(t).start()
    for t in range(size):
        other = (place + t) % size
        columns = pl.ds(pl.multiple_of(other * width, 128), width)
        mine = own[:, 0, :, columns].reshape(width, width)
        if t == 0:
            theirs = mine
        else:
            copy(size - t).wait_recv()
            theirs = landed[t].reshape(width, width).astype(jnp.float32)
        block[:, columns] = 0.5 * (mine + theirs.T)
    for t in range(1, size):
        copy(t).wait_send()


def local(count, near_blocks, diag_blocks, bases, leaf_nbrs, parent_nbrs):
    per_device, leaf_rows = bases.shape[0], bases.shape[1]
    red = leaf_rows - RANK
    slots = near_blocks.shape[1]
    targets = parent_nbrs.shape[1]
    span = REACH // per_device
    chips = (span + 1) // 2
    vmem = pl.BlockSpec(memory_space=pltpu.VMEM)
    anywhere = pl.BlockSpec(memory_space=pl.ANY)
    f32, bf16 = jnp.float32, jnp.bfloat16

    def out(shape, dtype):
        return jax.ShapeDtypeStruct(shape, dtype)

    group = 4
    steps = -(-slots // group)
    window = 2 * (2 * chips + 1)
    sems = pltpu.SemaphoreType.DMA((2, 2 * chips + 1))
    leaf_sems = pltpu.SemaphoreType.DMA((per_device,))
    factor, panel, skeleton, shift_t2, halves, win_bases, win_shift = pl.pallas_call(
        functools.partial(window_kernel, chips, count),
        out_shape=(
            out((per_device, red, red), f32),
            out((per_device, red, RANK), f32),
            out((per_device, RANK, RANK), f32),
            out((per_device, RANK, 2 * red), bf16),
            out((per_device, steps * group) + near_blocks.shape[2:], bf16),
            out((window,) + bases.shape, bf16),
            out((window, per_device, red, RANK), bf16),
        ),
        in_specs=[vmem, vmem, anywhere],
        out_specs=(vmem,) * 4 + (anywhere,) * 3,
        scratch_shapes=[
            pltpu.VMEM((per_device, red, RANK), bf16),
            pltpu.VMEM(bases.shape, bf16),
            pltpu.VMEM((per_device, red, 2 * red + RANK), f32),
            pltpu.VMEM((per_device, red, 2 * red + RANK), f32),
            pltpu.VMEM(near_blocks.shape, bf16),
            pltpu.VMEM(near_blocks.shape, bf16),
            sems,
            sems,
            sems,
            sems,
            pltpu.SemaphoreType.DMA((2,)),
            leaf_sems,
            leaf_sems,
        ],
        compiler_params=pltpu.CompilerParams(
            collective_id=0, has_side_effects=True, vmem_limit_bytes=66_000_000
        ),
        name="window",
    )(diag_blocks, bases, near_blocks)

    where = lax.axis_index("leaf").astype(jnp.int32).reshape(1)

    def half_map(leaf, step, where, nbrs, parents):
        return leaf, jnp.where(nbrs[leaf, step * group] >= 0, step, 0), 0, 0

    def by_leaf(rank):
        return lambda leaf, step, *_: (leaf,) + (0,) * (rank - 1)

    merged, diagonal = pl.pallas_call(
        functools.partial(couple_kernel, chips, group, slots),
        out_shape=(
            out((per_device, targets, RANK, CHILDREN * RANK), f32),
            out((per_device, RANK, CHILDREN * RANK), bf16),
        ),
        grid_spec=pltpu.PrefetchScalarGridSpec(
            num_scalar_prefetch=3,
            grid=(per_device, steps),
            in_specs=[
                pl.BlockSpec((1, group, leaf_rows, leaf_rows), half_map),
                pl.BlockSpec((1, RANK, 2 * red), by_leaf(3)),
                pl.BlockSpec((1, RANK, RANK), by_leaf(3)),
                vmem,
                vmem,
            ],
            out_specs=(
                pl.BlockSpec((1, targets, RANK, CHILDREN * RANK), by_leaf(4)),
                pl.BlockSpec((1, RANK, CHILDREN * RANK), by_leaf(3)),
            ),
        ),
        compiler_params=pltpu.CompilerParams(
            dimension_semantics=("arbitrary", "arbitrary"), vmem_limit_bytes=66_000_000
        ),
        name="couple",
    )(where, leaf_nbrs, parent_nbrs, halves, shift_t2, skeleton, win_bases, win_shift)

    size = CHILDREN // per_device
    width = per_device * RANK
    parent_block = pl.pallas_call(
        functools.partial(parent_kernel, size),
        out_shape=out((width, CHILDREN * RANK), f32),
        grid=(1,),
        in_specs=[
            pl.BlockSpec((per_device, 1, RANK, CHILDREN * RANK), lambda i: (0, 0, 0, 0)),
            vmem,
        ],
        out_specs=vmem,
        scratch_shapes=[
            pltpu.VMEM((size, per_device, RANK, width), bf16),
            pltpu.SemaphoreType.DMA((size,)),
            pltpu.SemaphoreType.DMA((size,)),
        ],
        compiler_params=pltpu.CompilerParams(collective_id=1, has_side_effects=True),
        name="parent",
    )(merged, diagonal)
    return factor, panel, merged, parent_block


def solution(mesh):
    count = mesh.shape["leaf"]
    in_specs = (
        P("leaf", None, None, None),
        P("leaf", None, None),
        P("leaf", None, None),
        P("leaf", None),
        P(),
    )
    out_specs = (
        P("leaf", None, None),
        P("leaf", None, None),
        P("leaf", None, None, None),
        P("leaf", None),
    )
    return jax.shard_map(
        functools.partial(local, count),
        mesh=mesh,
        in_specs=in_specs,
        out_specs=out_specs,
        check_vma=False,
    )
```

profile of v0, /device:TPU:17, one launch (start us, length us, event | category | flops | bytes accessed | tf_op | source)
XLA Modules:
  0.0 78.2 jit_solution(2460821973233992953)
XLA Ops:
  0.6 43.2 %window.1 = (f32[2,128,128]{2,1,0:T(8,128)}, f32[2,128,128]{2,1,0:T(8,128)}, f32[2,128,128]{2,1,0:T(8,128)}, bf16[2,128,256]{2,1,0:T(8,128)(2,1)}, bf16[2,28,256...) custom-call(bf16[2,256,256]{2,1,0:T(8,128)(2,1)} %diag.1, ...), custom_call_target="tpu_custom_call" | custom-call | tf_op jit(solution)/shard_map/window/pallas_call | solution.py:377
  43.8 19.0 %couple.1 = (f32[2,5,128,1024]{3,2,1,0:T(8,128)}, bf16[2,128,1024]{2,1,0:T(8,128)(2,1)}) custom-call(s32[1]{0:T(128)} %bitcast.where, s32[2,26]{1,0:T(2,128)} %nbrs.1, s32[8,5]{1,0:T(8,128)} %parents.1, bf16[2,28,256,256]{3,2,1,0:T(8,128)(2,1)} %get-tuple-element.15.halves, bf16[2,128,256]{2,1,0:T(8,128)(2,1)} %get-tuple-element.16.shift_t2, ...), custom_call_target="tpu_custom_call" | custom-call | tf_op jit(solution)/shard_map/couple/pallas_call | solution.py:419
  62.8 0.0 copy-start.1
  62.8 0.0 copy-start
  62.8 11.7 %parent.1 = f32[256,1024]{1,0:T(8,128)} custom-call(f32[2,5,128,1024]{3,2,1,0:T(8,128)} %get-tuple-element.28.own, bf16[2,128,1024]{2,1,0:T(8,128)(2,1)} %get-tuple-element.21.diagonal), custom_call_target="tpu_custom_call" | custom-call | tf_op jit(solution)/shard_map/parent/pallas_call | solution.py:448
  74.5 0.0 copy-done.1
  74.6 0.7 copy.12
  75.2 0.0 copy-done
  75.2 0.7 copy.13
  75.9 2.3 %copy.14 = f32[256,1024]{1,0:T(8,128)} copy(f32[256,1024]{1,0:T(8,128)} %parent.1) | data formatting | bytes 2097152
Async XLA Ops:
  62.8 11.7 %copy-start.1 = (f32[2,128,128]{2,1,0:T(8,128)S(1)}, f32[2,128,128]{2,1,0:T(8,128)}, u32[]{:S(2)}) copy-start(f32[2,128,128]{2,1,0:T(8,128)} %get-tuple-element.26) | copy-start | bytes 393220
  62.8 12.4 %copy-start = (f32[2,128,128]{2,1,0:T(8,128)S(1)}, f32[2,128,128]{2,1,0:T(8,128)}, u32[]{:S(2)}) copy-start(f32[2,128,128]{2,1,0:T(8,128)} %get-tuple-element.27) | copy-start | bytes 393220
where the time goes:
time: 78.4 us; the launch traced here: 78.2 us
  Pallas kernels  73.9 us (94%)
  local copies, waits for them, and re-layouts  3.63 us (5%)
    pallas_call x1, Pallas kernels, local(): pl.pallas_call(functools.partial(window_kernel, chips, count), out_shape=...  43.2 us
    pallas_call x1, Pallas kernels, local(): pl.pallas_call(functools.partial(couple_kernel, chips, group, slots), out...  19 us
    pallas_call x1, Pallas kernels, local(): pl.pallas_call(functools.partial(parent_kernel, size), out_shape=out((wid...  11.7 us
    unnamed x7, local copies, waits for them, and re-layouts  3.63 us

commit v1 on v0

v1 whole, which is shorter than its diff:
```python
import functools

import jax
import jax.numpy as jnp
from jax import lax
from jax.experimental import pallas as pl
from jax.experimental.pallas import tpu as pltpu
from jax.sharding import PartitionSpec as P

RANK = 128
REACH = 16
CHILDREN = 8
PANEL = 32
PLANE = 4
LINKS = ("x", "y", "up", "down")
MESH = pl.DeviceIdType.MESH
highest = lax.Precision.HIGHEST


def matmul(a, b):
    return jnp.dot(a, b, preferred_element_type=jnp.float32)


def matmul_t(a, b, precision=None):
    return lax.dot_general(
        a, b, (((0,), (0,)), ((), ())), preferred_element_type=jnp.float32, precision=precision
    )


def plan():
    def both(plane, chip):
        return [(plane, chip, 0), (plane, chip, 1)]

    inbound = (
        {
            "x": both(0, 1) + [(0, 3, 0)] + both(-1, 1),
            "y": both(0, 2) + [(0, 3, 1)] + both(-1, 2),
            "up": both(-1, 0) + both(-1, 3),
            "down": both(1, 0),
        },
        {
            "x": both(0, 0) + both(0, 2),
            "y": both(0, 3) + both(-1, 3),
            "up": both(-1, 1) + both(-1, 2),
            "down": both(1, 1) + both(1, 0),
        },
        {
            "x": both(0, 3) + both(0, 1),
            "y": both(0, 0) + both(1, 0),
            "up": both(-1, 2) + both(-1, 3),
            "down": both(1, 2) + both(1, 1),
        },
        {
            "x": both(0, 2) + [(0, 0, 0)] + both(1, 2),
            "y": both(0, 1) + [(0, 0, 1)] + both(1, 1),
            "up": both(-1, 3),
            "down": both(1, 3) + both(1, 0),
        },
    )
    outbound = []
    for place in range(PLANE):
        out = {"x": inbound[place ^ 1]["x"], "y": inbound[place ^ 2]["y"]}
        out["up"] = [(plane + 1, chip, leaf) for plane, chip, leaf in inbound[place]["up"]]
        out["down"] = [(plane - 1, chip, leaf) for plane, chip, leaf in inbound[place]["down"]]
        outbound.append(out)
    held = [{(0, place, leaf): 0 for leaf in range(2)} for place in range(PLANE)]
    arrivals = [[] for _ in range(PLANE)]
    queue = {(place, link): 0 for place in range(PLANE) for link in LINKS}
    now = 0
    while any(queue[place, link] < len(outbound[place][link]) for place, link in queue):
        now += 1
        landed = []
        for (place, link), done in queue.items():
            items = outbound[place][link]
            if done < len(items) and held[place].get(items[done], now) < now:
                target = {"x": place ^ 1, "y": place ^ 2}.get(link, place)
                landed.append((target, inbound[target][link][done]))
                queue[place, link] = done + 1
        for target, item in landed:
            held[target][item] = now
            arrivals[target].append((now, item))
    return outbound, arrivals


OUTBOUND, ARRIVALS = plan()
STEPS = max(now for events in ARRIVALS for now, _ in events)


def shift_of(place, item):
    plane, chip, _ = item
    return PLANE * plane + chip - place


def chunk_order(place):
    ready = {0: 0}
    for now, item in ARRIVALS[place]:
        ready[shift_of(place, item)] = now
    first = (0, (place ^ 1) - place)
    rest = sorted((now, delta) for delta, now in ready.items() if delta not in first)
    return list(first) + [delta for _, delta in rest], [ready[first[1]]] + [now for now, _ in rest]


def eliminate(diag, bases, factor, panel, skeleton, shift, bases_t, work, rows, prepare, serve):
    per_device, leaf_rows = bases.shape[0], bases.shape[1]
    red = leaf_rows - RANK
    wide = 2 * red + RANK
    row_id = lax.broadcasted_iota(jnp.int32, (red, red), 0)
    col_id = lax.broadcasted_iota(jnp.int32, (red, red), 1)
    low_corner = []
    for leaf in range(per_device):
        basis = bases[leaf]
        basis_t = basis.T
        bases_t[leaf] = basis_t
        half = matmul(basis_t, diag[leaf]).astype(jnp.bfloat16)
        dense = matmul(half, basis)
        top = dense[:red, :red]
        work[leaf, :, :red] = 0.5 * (top + top.T)
        work[leaf, :, red : red + RANK] = dense[:red, red:]
        work[leaf, :, red + RANK :] = (row_id == col_id).astype(jnp.float32)
        low_corner.append(dense[red:, red:])
    prepare()
    sub = lax.broadcasted_iota(jnp.int32, (PANEL, 1), 0)
    for start in range(0, red, PANEL):
        strips = [work[leaf, start : start + PANEL, :] for leaf in range(per_device)]
        for k in range(PANEL):
            for leaf in range(per_device):
                strip = strips[leaf]
                column = strip[:, start + k : start + k + 1]
                ratio = jnp.where(sub > k, column / column[k : k + 1], 0.0)
                strips[leaf] = strip - ratio * strip[k : k + 1, :]
        lane = lax.broadcasted_iota(jnp.int32, (PANEL, wide), 1)
        line = lax.broadcasted_iota(jnp.int32, (PANEL, wide), 0)
        for leaf in range(per_device):
            strip = strips[leaf]
            pivots = jnp.sum(jnp.where(lane == line + start, strip, 0.0), axis=1, keepdims=True)
            strip = strip * (1.0 / jnp.sqrt(pivots))
            rows[leaf, start : start + PANEL, :] = strip
            if start + PANEL < red:
                work[leaf] = work[leaf] - matmul_t(strip[:, :red], strip, highest)
        serve(start + PANEL)
    for leaf in range(per_device):
        solved = rows[leaf, :, red : red + RANK]
        inverse = jnp.where(col_id <= row_id, rows[leaf, :, red + RANK :], 0.0)
        shift[leaf] = matmul_t(inverse, solved, highest).astype(jnp.bfloat16)
    serve(red + 1)
    for leaf in range(per_device):
        solved = rows[leaf, :, red : red + RANK]
        panel[leaf] = solved
        skeleton[leaf] = low_corner[leaf] - matmul_t(solved, solved, highest)
        upper = jnp.where(col_id >= row_id, rows[leaf, :, :red], 0.0)
        factor[leaf] = upper.T


def split(values):
    high = values.astype(jnp.bfloat16)
    return high, (values - high.astype(jnp.float32)).astype(jnp.bfloat16)


def level_kernel(
    count,
    parents,
    targets,
    nbrs,
    diag,
    bases,
    near,
    factor,
    panel,
    blocks,
    landed,
    win_bases,
    win_shift,
    shift,
    skeleton,
    bases_t,
    work,
    rows,
    near_in,
    sides,
    diagonal,
    send,
    recv,
    pass_send,
    pass_recv,
    own_sem,
    near_sem,
    row_send,
    row_recv,
    found,
    lookup,
    found_sem,
):
    per_device, slots = near_in.shape[0], near_in.shape[1]
    red = shift.shape[1]
    total = count // 2
    me = lax.axis_index("leaf")
    core, chip = me % 2, me // 2
    sibling = me + 1 - 2 * core
    place = chip % PLANE
    size = CHILDREN // per_device
    seat = me % size
    across = me + 2 * (1 - 2 * (place % 2))
    along = me + 4 * (1 - 2 * (place // 2))
    device = {"x": across, "y": along, "up": me + 2 * PLANE, "down": me - 2 * PLANE}
    present = {"up": chip + PLANE < total, "down": chip - PLANE >= 0}
    far = across + 1 - 2 * core

    fetches = [
        pltpu.make_async_copy(near.at[leaf], near_in.at[leaf], near_sem.at[leaf])
        for leaf in range(per_device)
    ]
    for fetch in fetches:
        fetch.start()

    barrier = pltpu.get_barrier_semaphore()
    for other in (sibling, across, along, far):
        pl.semaphore_signal(barrier, inc=1, device_id=(other,), device_id_type=MESH)
    peers = jnp.int32(4)
    for link in ("up", "down"):

        @pl.when(present[link])
        def _(link=link):
            pl.semaphore_signal(barrier, inc=1, device_id=(device[link],), device_id_type=MESH)

        peers = peers + present[link].astype(jnp.int32)

    pairs = ((bases, win_bases), (shift, win_shift))

    def exists(delta):
        return (chip + delta >= 0) & (chip + delta < total)

    def slot_of(delta, holder):
        return 2 * (PLANE + delta) + holder

    def hop(kind, at, link, order):
        item = OUTBOUND[at][link][order]
        delta = shift_of(at, item)
        moved = {"x": at - (at ^ 1), "y": at - (at ^ 2), "up": -PLANE, "down": PLANE}[link]
        source, window = pairs[kind]
        leaf = item[2]
        return pltpu.make_async_remote_copy(
            src_ref=source.at[leaf] if delta == 0 else window.at[slot_of(delta, core), leaf],
            dst_ref=window.at[slot_of(delta + moved, core), leaf],
            send_sem=send.at[kind, LINKS.index(link), order],
            recv_sem=recv.at[kind, PLANE + delta + moved, leaf],
            device_id=(device[link],),
            device_id_type=MESH,
        )

    def arrival(kind, delta, leaf):
        window = pairs[kind][1]
        there = window.at[slot_of(delta, core), leaf]
        return pltpu.make_async_remote_copy(
            src_ref=there,
            dst_ref=there,
            send_sem=send.at[kind, 0, 0],
            recv_sem=recv.at[kind, PLANE + delta, leaf],
            device_id=(sibling,),
            device_id_type=MESH,
        )

    def relay(kind, delta, leaf, own=False):
        source, window = pairs[kind]
        there = window.at[slot_of(delta, core), leaf]
        return pltpu.make_async_remote_copy(
            src_ref=source.at[leaf] if own else there,
            dst_ref=there,
            send_sem=pass_send.at[kind, PLANE + delta, leaf],
            recv_sem=pass_recv.at[kind, PLANE + delta, leaf],
            device_id=(sibling,),
            device_id_type=MESH,
        )

    def relayed(kind, delta, leaf):
        window = pairs[kind][1]
        there = window.at[slot_of(delta, 1 - core), leaf]
        return pltpu.make_async_remote_copy(
            src_ref=there,
            dst_ref=there,
            send_sem=pass_send.at[kind, PLANE + delta, leaf],
            recv_sem=pass_recv.at[kind, PLANE + delta, leaf],
            device_id=(sibling,),
            device_id_type=MESH,
        )

    def on_links(kind, at, item, act):
        for link in LINKS:
            for order, entry in enumerate(OUTBOUND[at][link]):
                if entry == item:
                    if link in present:
                        pl.when(present[link])(lambda: act(hop(kind, at, link, order)))
                    else:
                        act(hop(kind, at, link, order))

    def start(copy):
        copy.start()

    def stop(copy):
        copy.wait_send()

    def own_copy(kind):
        source, window = pairs[kind]
        return pltpu.make_async_copy(source, window.at[slot_of(0, core)], own_sem.at[kind])

    def by_place(act):
        for at in range(PLANE):
            pl.when(place == at)(lambda: act(at))

    def dispatch(kind):
        def act(at):
            for leaf in range(per_device):
                on_links(kind, at, (0, at, leaf), start)

        by_place(act)
        for leaf in range(per_device):
            relay(kind, 0, leaf, own=True).start()
        own_copy(kind).start()

    def serve(kind, step):
        def act(at):
            for now, item in ARRIVALS[at]:
                if now == step:
                    delta, leaf = shift_of(at, item), item[2]

                    def one():
                        arrival(kind, delta, leaf).wait_recv()
                        on_links(kind, at, item, start)
                        relay(kind, delta, leaf).start()

                    if item[0] == 0:
                        one()
                    else:
                        pl.when(exists(delta))(one)

        by_place(act)

    def finish(kind):
        def act(at):
            for leaf in range(per_device):
                on_links(kind, at, (0, at, leaf), stop)
            for _, item in ARRIVALS[at]:
                delta, leaf = shift_of(at, item), item[2]

                def one():
                    on_links(kind, at, item, stop)
                    relay(kind, delta, leaf).wait_send()

                if item[0] == 0:
                    one()
                else:
                    pl.when(exists(delta))(one)

        by_place(act)
        for leaf in range(per_device):
            relay(kind, 0, leaf, own=True).wait_send()

    number = me * per_device
    parent = number // CHILDREN
    low = jnp.clip(parent - targets // 2, 0, parents - targets)
    home = parent - low
    blocks[...] = jnp.zeros_like(blocks)
    reach = found.shape[1]
    offset = lax.broadcasted_iota(jnp.int32, (reach, slots), 0) - reach // 2
    order = lax.broadcasted_iota(jnp.int32, (reach, slots), 1)
    for leaf in range(per_device):
        away = offset + number + leaf
        hit = (nbrs[leaf : leaf + 1, :] == away) & (away >= 0)
        slot = jnp.max(jnp.where(hit, order, -1), axis=1, keepdims=True)
        found[leaf] = jnp.broadcast_to(slot, found.shape[1:])
    table = pltpu.make_async_copy(found, lookup, found_sem)
    table.start()

    def prepare():
        pl.semaphore_wait(barrier, peers)
        dispatch(0)

    def between(point):
        panels = red // PANEL
        if point <= red:
            serve(0, point // PANEL)
        else:
            dispatch(1)

    eliminate(diag, bases, factor, panel, skeleton, shift, bases_t, work, rows, prepare, between)
    for step in range(red // PANEL + 1, STEPS + 1):
        serve(0, step)
    for fetch in fetches:
        fetch.wait()

    unroll = max(n for n in range(1, 14) if slots % n == 0)

    @pl.loop(0, slots // unroll)
    def _(turn):
        for k in range(unroll):
            n = turn * unroll + k
            for leaf in range(per_device):
                half = matmul(bases_t[leaf], near_in[leaf, n]).astype(jnp.bfloat16)
                high, low_part = split(-matmul_t(shift[leaf], half[:red]))
                sides[leaf, n, :, : 2 * RANK] = half[red:]
                sides[leaf, n, :, 2 * RANK : 4 * RANK] = high
                sides[leaf, n, :, 4 * RANK :] = low_part

    table.wait()
    own_copy(0).wait()
    own_copy(1).wait()

    orders = [chunk_order(at) for at in range(PLANE)]

    def pick(values):
        chosen = jnp.int32(values[0])
        for at in range(1, PLANE):
            chosen = jnp.where(place == at, jnp.int32(values[at]), chosen)
        return chosen

    def couple(delta):
        for kind in range(2):
            for leaf in range(per_device):
                relayed(kind, delta, leaf).wait_recv()
        for holder in range(2):
            for leaf in range(per_device):
                slot = slot_of(delta, holder)
                basis = win_bases[slot, leaf]
                moved = win_shift[slot, leaf]
                outer = basis[:, red:]
                change = outer.astype(jnp.float32) - matmul(basis[:, :red], moved)
                high, low_part = split(change)
                right = jnp.concatenate([high, low_part, outer, outer], axis=0)
                other = ((chip + delta) * 2 + holder) * per_device + leaf
                left = []
                live = []
                for mine in range(per_device):
                    n = lookup[mine, other - number - mine + REACH + CHILDREN, 0]
                    side = sides[mine, jnp.maximum(n, 0)]
                    left.append(jnp.concatenate([side[:, : 2 * RANK], side], axis=1))
                    live.append(n >= 0)
                schur = matmul(jnp.concatenate(left, axis=0), right)
                column = pl.multiple_of((other % CHILDREN) * RANK, RANK)
                row = other // CHILDREN - low
                for mine in range(per_device):
                    apart = other - number - mine
                    value = jnp.where(live[mine], schur[mine * RANK : (mine + 1) * RANK], 0.0)

                    @pl.when((apart <= REACH) & (apart >= -REACH))
                    def _(mine=mine, value=value):
                        blocks[mine, row, :, pl.ds(column, RANK)] = value

    def row_copy(t):
        other = (seat + t) % size
        width = per_device * RANK
        return pltpu.make_async_remote_copy(
            src_ref=diagonal.at[:, :, pl.ds(pl.multiple_of(other * width, 128), width)],
            dst_ref=landed.at[size - t],
            send_sem=row_send.at[t],
            recv_sem=row_recv.at[size - t],
            device_id=(me - seat + other,),
            device_id_type=MESH,
        )

    served = 0
    chunks = len(orders[0][0])
    for turn in range(chunks):
        if turn:
            needed = max(order[1][turn - 1] for order in orders)
            while served < needed:
                served += 1
                serve(1, served)
        delta = pick([order[0][turn] for order in orders])
        pl.when(exists(delta))(lambda: couple(delta))
        if turn == 0:
            for leaf in range(per_device):
                column = pl.multiple_of(((number + leaf) % CHILDREN) * RANK, RANK)
                blocks[leaf, home, :, pl.ds(column, RANK)] = skeleton[leaf]
        if turn == 1:
            for leaf in range(per_device):
                diagonal[leaf] = blocks[leaf, home].astype(jnp.bfloat16)
            for t in range(1, size):
                row_copy(t).start()

    finish(0)
    finish(1)
    for t in range(1, size):
        row_copy(size - t).wait_recv()
    for t in range(1, size):
        row_copy(t).wait_send()


def place_kernel(
    parents, factor, panel, blocks, landed, factor_out, panel_out, merged, block_out, block, sems
):
    per_device, targets = blocks.shape[0], blocks.shape[1]
    size = landed.shape[0]
    width = per_device * RANK
    me = lax.axis_index("leaf")
    seat = me % size
    parent = me * per_device // CHILDREN
    low = jnp.clip(parent - targets // 2, 0, parents.shape[0] - targets)
    copies = []

    def put(source, target):
        copy = pltpu.make_async_copy(source, target, sems.at[len(copies)])
        copy.start()
        copies.append(copy)

    for q in range(targets):
        row = parents[parent, q] - low
        for leaf in range(per_device):
            put(blocks.at[leaf, row], merged.at[leaf, q])
    put(factor, factor_out)
    put(panel, panel_out)
    for t in range(size):
        columns = pl.ds(pl.multiple_of(((seat + t) % size) * width, 128), width)
        mine = blocks[:, parent - low, :, columns].reshape(width, width)
        if t == 0:
            theirs = mine
        else:
            theirs = landed[t].reshape(width, width).astype(jnp.float32)
        block[:, columns] = 0.5 * (mine + theirs.T)
        put(block.at[:, columns], block_out.at[:, columns])
    for copy in copies:
        copy.wait()


def local(count, near_blocks, diag_blocks, bases, leaf_nbrs, parent_nbrs):
    per_device, leaf_rows = bases.shape[0], bases.shape[1]
    red = leaf_rows - RANK
    slots = near_blocks.shape[1]
    parents, targets = parent_nbrs.shape
    assert per_device == 2 and REACH == 4 * PLANE
    vmem = pl.BlockSpec(memory_space=pltpu.VMEM)
    smem = pl.BlockSpec(memory_space=pltpu.SMEM)
    hbm = pl.BlockSpec(memory_space=pltpu.HBM)
    f32, bf16 = jnp.float32, jnp.bfloat16

    def out(shape, dtype):
        return jax.ShapeDtypeStruct(shape, dtype)

    reach = 2 * (REACH + CHILDREN)
    size = CHILDREN // per_device
    width = per_device * RANK
    window = 2 * (2 * PLANE + 1)
    links = max(len(out_[link]) for out_ in OUTBOUND for link in LINKS)
    sems = pltpu.SemaphoreType.DMA
    factor, panel, blocks, landed = pl.pallas_call(
        functools.partial(level_kernel, count, parents, targets),
        out_shape=(
            out((per_device, red, red), f32),
            out((per_device, red, RANK), f32),
            out((per_device, targets, RANK, CHILDREN * RANK), f32),
            out((size, per_device, RANK, width), bf16),
        ),
        in_specs=[vmem, vmem, vmem, hbm],
        out_specs=(vmem,) * 4,
        scratch_shapes=[
            pltpu.VMEM((window,) + bases.shape, bf16),
            pltpu.VMEM((window, per_device, red, RANK), bf16),
            pltpu.VMEM((per_device, red, RANK), bf16),
            pltpu.VMEM((per_device, RANK, RANK), f32),
            pltpu.VMEM(bases.shape, bf16),
            pltpu.VMEM((per_device, red, 2 * red + RANK), f32),
            pltpu.VMEM((per_device, red, 2 * red + RANK), f32),
            pltpu.VMEM(near_blocks.shape, bf16),
            pltpu.VMEM((per_device, slots, RANK, 6 * RANK), bf16),
            pltpu.VMEM((per_device, RANK, CHILDREN * RANK), bf16),
            sems((2, len(LINKS), links)),
            sems((2, 2 * PLANE + 1, per_device)),
            sems((2, 2 * PLANE + 1, per_device)),
            sems((2, 2 * PLANE + 1, per_device)),
            sems((2,)),
            sems((per_device,)),
            sems((size,)),
            sems((size,)),
            pltpu.VMEM((per_device, reach, 128), jnp.int32),
            pltpu.SMEM((per_device, reach, 128), jnp.int32),
            sems(()),
        ],
        compiler_params=pltpu.CompilerParams(
            collective_id=0, has_side_effects=True, vmem_limit_bytes=46_500_000
        ),
        name="level",
    )(leaf_nbrs, diag_blocks, bases, near_blocks)

    return pl.pallas_call(
        place_kernel,
        out_shape=(
            out((per_device, red, red), f32),
            out((per_device, red, RANK), f32),
            out((per_device, targets, RANK, CHILDREN * RANK), f32),
            out((width, CHILDREN * RANK), f32),
        ),
        in_specs=[smem, vmem, vmem, vmem, vmem],
        out_specs=(hbm,) * 4,
        scratch_shapes=[
            pltpu.VMEM((width, CHILDREN * RANK), f32),
            sems((targets * per_device + 2 + size,)),
        ],
        compiler_params=pltpu.CompilerParams(vmem_limit_bytes=16_000_000),
        name="place",
    )(parent_nbrs, factor, panel, blocks, landed)


def solution(mesh):
    count = mesh.shape["leaf"]
    in_specs = (
        P("leaf", None, None, None),
        P("leaf", None, None),
        P("leaf", None, None),
        P("leaf", None),
        P(),
    )
    out_specs = (
        P("leaf", None, None),
        P("leaf", None, None),
        P("leaf", None, None, None),
        P("leaf", None),
    )
    return jax.shard_map(
        functools.partial(local, count),
        mesh=mesh,
        in_specs=in_specs,
        out_specs=out_specs,
        check_vma=False,
    )
```

time: 78.4 us -> 63 us (0.80)
  the two profiles are of different devices: /device:TPU:17 before, /device:TPU:7 now
where the time goes in v1:
time: 63 us; the launch traced here: 62.8 us
  Pallas kernels  59.4 us (94%)
  local copies, waits for them, and re-layouts  2.57 us (4%)
  between operations  0.82 us (1%)
    pallas_call x1, Pallas kernels, local(): pl.pallas_call(functools.partial(level_kernel, count, parents, targets),...  55.9 us
    pallas_call x1, Pallas kernels, local(): pl.pallas_call(place_kernel, out_shape=(out((per_device, red, red), f32),...  3.49 us
    unnamed x8, local copies, waits for them, and re-layouts  2.57 us

profile of v1, /device:TPU:7, one launch (start us, length us, event | category | flops | bytes accessed | tf_op | source)
XLA Modules:
  0.0 62.8 jit_solution(14464900528012101587)
XLA Ops:
  0.6 0.0 copy-start
  0.6 0.9 %copy-done = bf16[2,256,256]{2,1,0:T(8,128)(2,1)S(1)} copy-done((bf16[2,256,256]{2,1,0:T(8,128)(2,1)S(1)}, bf16[2,256,256]{2,1,0:T(8,128)(2,1)}, u32[]{:S(2)}) %copy-start) | copy-done | bytes 262168
  1.6 0.0 copy-start.1
  1.6 0.9 %copy-done.1 = bf16[2,256,256]{2,1,0:T(8,128)(2,1)S(1)} copy-done((bf16[2,256,256]{2,1,0:T(8,128)(2,1)S(1)}, bf16[2,256,256]{2,1,0:T(8,128)(2,1)}, u32[]{:S(2)}) %copy-start.1) | copy-done | bytes 262168
  2.5 0.0 copy-start.3
  2.5 0.7 %copy-done.3 = s32[2,26]{1,0:T(2,128)S(1)} copy-done((s32[2,26]{1,0:T(2,128)S(1)}, s32[2,26]{1,0:T(2,128)}, u32[]{:S(2)}) %copy-start.3) | copy-done | bytes 232
  3.2 0.0 copy-start.2
  3.2 55.9 %level.1 = (f32[2,128,128]{2,1,0:T(8,128)S(1)}, f32[2,128,128]{2,1,0:T(8,128)S(1)}, f32[2,5,128,1024]{3,2,1,0:T(8,128)S(1)}, bf16[4,2,128,256]{3,2,1,0:T(8,128)(2,1)S(1)}) custom-call(s32[2,26]{1,0:T(2,128)S(1)} %copy-done.3, bf16[2,256,256]{2,1,0:T(8,128)(2,1)S(1)} %copy-done, bf16[2,256,256]{2,1,0:T(8,128)(2,1)S(1)} %copy-done.1, ...), custom_call_target="tpu_custom_call" | custom-call | tf_op jit(solution)/shard_map/level/pallas_call | solution.py:543
  59.1 0.0 copy-done.2
  59.1 3.5 %place.1 = (f32[2,128,128]{2,1,0:T(8,128)}, f32[2,128,128]{2,1,0:T(8,128)}, f32[2,5,128,1024]{3,2,1,0:T(8,128)}, f32[256,1024]{1,0:T(8,128)}) custom-call(s32[8,5]{1,0:T(8,128)S(1)} %copy-done.2, f32[2,128,128]{2,1,0:T(8,128)S(1)} %get-tuple-element.8.factor, f32[2,128,128]{2,1,0:T(8,128)S(1)} %get-tuple-element.9.panel, ...), custom_call_target="tpu_custom_call" | custom-call | tf_op jit(solution)/shard_map/place/pallas_call | solution.py:582
Async XLA Ops:
  0.6 1.0 %copy-start = (bf16[2,256,256]{2,1,0:T(8,128)(2,1)S(1)}, bf16[2,256,256]{2,1,0:T(8,128)(2,1)}, u32[]{:S(2)}) copy-start(bf16[2,256,256]{2,1,0:T(8,128)(2,1)} %diag.1) | copy-start | bytes 786436
  1.6 0.9 %copy-start.1 = (bf16[2,256,256]{2,1,0:T(8,128)(2,1)S(1)}, bf16[2,256,256]{2,1,0:T(8,128)(2,1)}, u32[]{:S(2)}) copy-start(bf16[2,256,256]{2,1,0:T(8,128)(2,1)} %bases.1) | copy-start | bytes 786436
  2.5 0.7 %copy-start.3 = (s32[2,26]{1,0:T(2,128)S(1)}, s32[2,26]{1,0:T(2,128)}, u32[]{:S(2)}) copy-start(s32[2,26]{1,0:T(2,128)} %nbrs.1) | copy-start | bytes 628
  3.2 55.9 %copy-start.2 = (s32[8,5]{1,0:T(8,128)S(1)}, s32[8,5]{1,0:T(8,128)}, u32[]{:S(2)}) copy-start(s32[8,5]{1,0:T(8,128)} %parents.1) | copy-start | bytes 484

commit v2 on v1

--- a/solution.py
+++ b/solution.py
@@ -33,9 +33,9 @@
 
     inbound = (
         {
-            "x": both(0, 1) + [(0, 3, 0)] + both(-1, 1),
+            "x": both(0, 1) + [(0, 3, 0), (-1, 1, 0)],
             "y": both(0, 2) + [(0, 3, 1)] + both(-1, 2),
-            "up": both(-1, 0) + both(-1, 3),
+            "up": both(-1, 0) + [(-1, 1, 1)] + both(-1, 3),
             "down": both(1, 0),
         },
         {
@@ -51,10 +51,10 @@
             "down": both(1, 2) + both(1, 1),
         },
         {
-            "x": both(0, 2) + [(0, 0, 0)] + both(1, 2),
+            "x": both(0, 2) + [(0, 0, 0), (1, 2, 0)],
             "y": both(0, 1) + [(0, 0, 1)] + both(1, 1),
             "up": both(-1, 3),
-            "down": both(1, 3) + both(1, 0),
+            "down": both(1, 3) + [(1, 2, 1)] + both(1, 0),
         },
     )
     outbound = []
@@ -95,18 +95,17 @@
     ready = {0: 0}
     for now, item in ARRIVALS[place]:
         ready[shift_of(place, item)] = now
-    first = (0, (place ^ 1) - place)
+    first = [0, (place ^ 1) - place, (place ^ 2) - place, -PLANE, PLANE]
     rest = sorted((now, delta) for delta, now in ready.items() if delta not in first)
-    return list(first) + [delta for _, delta in rest], [ready[first[1]]] + [now for now, _ in rest]
-
-
-def eliminate(diag, bases, factor, panel, skeleton, shift, bases_t, work, rows, prepare, serve):
+    order = first + [delta for _, delta in rest]
+    return order, [ready[delta] for delta in order]
+
+
+def reduce_blocks(diag, bases, bases_t, work, low_corner):
     per_device, leaf_rows = bases.shape[0], bases.shape[1]
     red = leaf_rows - RANK
-    wide = 2 * red + RANK
     row_id = lax.broadcasted_iota(jnp.int32, (red, red), 0)
     col_id = lax.broadcasted_iota(jnp.int32, (red, red), 1)
-    low_corner = []
     for leaf in range(per_device):
         basis = bases[leaf]
         basis_t = basis.T
@@ -117,8 +116,14 @@
         work[leaf, :, :red] = 0.5 * (top + top.T)
         work[leaf, :, red : red + RANK] = dense[:red, red:]
         work[leaf, :, red + RANK :] = (row_id == col_id).astype(jnp.float32)
-        low_corner.append(dense[red:, red:])
-    prepare()
+        low_corner[leaf] = dense[red:, red:]
+
+
+def eliminate(shift, turned, work, rows, serve):
+    per_device, red = work.shape[0], work.shape[1]
+    wide = 2 * red + RANK
+    row_id = lax.broadcasted_iota(jnp.int32, (red, red), 0)
+    col_id = lax.broadcasted_iota(jnp.int32, (red, red), 1)
     sub = lax.broadcasted_iota(jnp.int32, (PANEL, 1), 0)
     for start in range(0, red, PANEL):
         strips = [work[leaf, start : start + PANEL, :] for leaf in range(per_device)]
@@ -137,12 +142,21 @@
             rows[leaf, start : start + PANEL, :] = strip
             if start + PANEL < red:
                 work[leaf] = work[leaf] - matmul_t(strip[:, :red], strip, highest)
-        serve(start + PANEL)
+        serve(start // PANEL)
     for leaf in range(per_device):
         solved = rows[leaf, :, red : red + RANK]
         inverse = jnp.where(col_id <= row_id, rows[leaf, :, red + RANK :], 0.0)
-        shift[leaf] = matmul_t(inverse, solved, highest).astype(jnp.bfloat16)
-    serve(red + 1)
+        moved = matmul_t(inverse, solved, highest)
+        shift[leaf] = moved.astype(jnp.bfloat16)
+        back = -moved.astype(jnp.bfloat16).astype(jnp.float32).T
+        turned[leaf, :, :red] = back.astype(jnp.bfloat16)
+        turned[leaf, :, red:] = back.astype(jnp.bfloat16)
+
+
+def finish_factor(factor, panel, skeleton, rows, low_corner):
+    per_device, red = rows.shape[0], rows.shape[1]
+    row_id = lax.broadcasted_iota(jnp.int32, (red, red), 0)
+    col_id = lax.broadcasted_iota(jnp.int32, (red, red), 1)
     for leaf in range(per_device):
         solved = rows[leaf, :, red : red + RANK]
         panel[leaf] = solved
@@ -170,19 +184,23 @@
     landed,
     win_bases,
     win_shift,
-    shift,
+    diag_in,
+    nbrs_in,
+    low_corner,
     skeleton,
+    turned,
     bases_t,
     work,
     rows,
     near_in,
-    sides,
+    halves,
+    lefts,
     diagonal,
     send,
     recv,
     pass_send,
     pass_recv,
-    own_sem,
+    in_sem,
     near_sem,
     row_send,
     row_recv,
@@ -191,7 +209,7 @@
     found_sem,
 ):
     per_device, slots = near_in.shape[0], near_in.shape[1]
-    red = shift.shape[1]
+    red = rows.shape[1]
     total = count // 2
     me = lax.axis_index("leaf")
     core, chip = me % 2, me // 2
@@ -209,8 +227,15 @@
         pltpu.make_async_copy(near.at[leaf], near_in.at[leaf], near_sem.at[leaf])
         for leaf in range(per_device)
     ]
-    for fetch in fetches:
-        fetch.start()
+    here = 2 * PLANE + core
+    inputs = [
+        pltpu.make_async_copy(source, target, in_sem.at[n])
+        for n, (source, target) in enumerate(
+            ((nbrs, nbrs_in), (bases, win_bases.at[here]), (diag, diag_in))
+        )
+    ]
+    for copy in inputs + fetches:
+        copy.start()
 
     barrier = pltpu.get_barrier_semaphore()
     for other in (sibling, across, along, far):
@@ -224,7 +249,7 @@
 
         peers = peers + present[link].astype(jnp.int32)
 
-    pairs = ((bases, win_bases), (shift, win_shift))
+    windows = (win_bases, win_shift)
 
     def exists(delta):
         return (chip + delta >= 0) & (chip + delta < total)
@@ -236,10 +261,10 @@
         item = OUTBOUND[at][link][order]
         delta = shift_of(at, item)
         moved = {"x": at - (at ^ 1), "y": at - (at ^ 2), "up": -PLANE, "down": PLANE}[link]
-        source, window = pairs[kind]
+        window = windows[kind]
         leaf = item[2]
         return pltpu.make_async_remote_copy(
-            src_ref=source.at[leaf] if delta == 0 else window.at[slot_of(delta, core), leaf],
+            src_ref=window.at[slot_of(delta, core), leaf],
             dst_ref=window.at[slot_of(delta + moved, core), leaf],
             send_sem=send.at[kind, LINKS.index(link), order],
             recv_sem=recv.at[kind, PLANE + delta + moved, leaf],
@@ -248,7 +273,7 @@
         )
 
     def arrival(kind, delta, leaf):
-        window = pairs[kind][1]
+        window = windows[kind]
         there = window.at[slot_of(delta, core), leaf]
         return pltpu.make_async_remote_copy(
             src_ref=there,
@@ -259,11 +284,11 @@
             device_id_type=MESH,
         )
 
-    def relay(kind, delta, leaf, own=False):
-        source, window = pairs[kind]
+    def relay(kind, delta, leaf):
+        window = windows[kind]
         there = window.at[slot_of(delta, core), leaf]
         return pltpu.make_async_remote_copy(
-            src_ref=source.at[leaf] if own else there,
+            src_ref=there,
             dst_ref=there,
             send_sem=pass_send.at[kind, PLANE + delta, leaf],
             recv_sem=pass_recv.at[kind, PLANE + delta, leaf],
@@ -272,7 +297,7 @@
         )
 
     def relayed(kind, delta, leaf):
-        window = pairs[kind][1]
+        window = windows[kind]
         there = window.at[slot_of(delta, 1 - core), leaf]
         return pltpu.make_async_remote_copy(
             src_ref=there,
@@ -298,10 +323,6 @@
     def stop(copy):
         copy.wait_send()
 
-    def own_copy(kind):
-        source, window = pairs[kind]
-        return pltpu.make_async_copy(source, window.at[slot_of(0, core)], own_sem.at[kind])
-
     def by_place(act):
         for at in range(PLANE):
             pl.when(place == at)(lambda: act(at))
@@ -313,8 +334,7 @@
 
         by_place(act)
         for leaf in range(per_device):
-            relay(kind, 0, leaf, own=True).start()
-        own_copy(kind).start()
+            relay(kind, 0, leaf).start()
 
     def serve(kind, step):
         def act(at):
@@ -352,59 +372,48 @@
 
         by_place(act)
         for leaf in range(per_device):
-            relay(kind, 0, leaf, own=True).wait_send()
+            relay(kind, 0, leaf).wait_send()
 
     number = me * per_device
     parent = number // CHILDREN
     low = jnp.clip(parent - targets // 2, 0, parents - targets)
     home = parent - low
     blocks[...] = jnp.zeros_like(blocks)
+    halves[:, slots] = jnp.zeros_like(halves[:, slots])
     reach = found.shape[1]
     offset = lax.broadcasted_iota(jnp.int32, (reach, slots), 0) - reach // 2
     order = lax.broadcasted_iota(jnp.int32, (reach, slots), 1)
+    inputs[0].wait()
     for leaf in range(per_device):
         away = offset + number + leaf
-        hit = (nbrs[leaf : leaf + 1, :] == away) & (away >= 0)
+        hit = (nbrs_in[leaf : leaf + 1, :] == away) & (away >= 0)
         slot = jnp.max(jnp.where(hit, order, -1), axis=1, keepdims=True)
-        found[leaf] = jnp.broadcast_to(slot, found.shape[1:])
+        found[leaf] = jnp.broadcast_to(jnp.where(slot < 0, slots, slot), found.shape[1:])
     table = pltpu.make_async_copy(found, lookup, found_sem)
     table.start()
-
-    def prepare():
-        pl.semaphore_wait(barrier, peers)
-        dispatch(0)
-
-    def between(point):
-        panels = red // PANEL
-        if point <= red:
-            serve(0, point // PANEL)
-        else:
-            dispatch(1)
-
-    eliminate(diag, bases, factor, panel, skeleton, shift, bases_t, work, rows, prepare, between)
-    for step in range(red // PANEL + 1, STEPS + 1):
-        serve(0, step)
-    for fetch in fetches:
-        fetch.wait()
+    for copy in inputs[1:]:
+        copy.wait()
+    reduce_blocks(diag_in, win_bases.at[here], bases_t, work, low_corner)
+    pl.semaphore_wait(barrier, peers)
+    dispatch(0)
+
+    def between(panel_done):
+        if panel_done > 0 and panel_done < red // PANEL - 1:
+            serve(0, panel_done)
+
+    eliminate(win_shift.at[here], turned, work, rows, between)
+    dispatch(1)
 
     unroll = max(n for n in range(1, 14) if slots % n == 0)
 
-    @pl.loop(0, slots // unroll)
-    def _(turn):
+    def project(turn):
         for k in range(unroll):
             n = turn * unroll + k
             for leaf in range(per_device):
-                half = matmul(bases_t[leaf], near_in[leaf, n]).astype(jnp.bfloat16)
-                high, low_part = split(-matmul_t(shift[leaf], half[:red]))
-                sides[leaf, n, :, : 2 * RANK] = half[red:]
-                sides[leaf, n, :, 2 * RANK : 4 * RANK] = high
-                sides[leaf, n, :, 4 * RANK :] = low_part
-
-    table.wait()
-    own_copy(0).wait()
-    own_copy(1).wait()
+                halves[leaf, n] = matmul(bases_t[leaf], near_in[leaf, n]).astype(jnp.bfloat16)
 
     orders = [chunk_order(at) for at in range(PLANE)]
+    chunks = len(orders[0][0])
 
     def pick(values):
         chosen = jnp.int32(values[0])
@@ -412,37 +421,80 @@
             chosen = jnp.where(place == at, jnp.int32(values[at]), chosen)
         return chosen
 
-    def couple(delta):
-        for kind in range(2):
-            for leaf in range(per_device):
-                relayed(kind, delta, leaf).wait_recv()
+    deltas = [pick([order[0][turn] for order in orders]) for turn in range(chunks)]
+    steps = [max(order[1][turn] for order in orders) for turn in range(chunks)]
+
+    def pairs_of(turn):
+        delta = deltas[turn]
         for holder in range(2):
             for leaf in range(per_device):
-                slot = slot_of(delta, holder)
-                basis = win_bases[slot, leaf]
-                moved = win_shift[slot, leaf]
-                outer = basis[:, red:]
-                change = outer.astype(jnp.float32) - matmul(basis[:, :red], moved)
-                high, low_part = split(change)
-                right = jnp.concatenate([high, low_part, outer, outer], axis=0)
                 other = ((chip + delta) * 2 + holder) * per_device + leaf
-                left = []
-                live = []
-                for mine in range(per_device):
-                    n = lookup[mine, other - number - mine + REACH + CHILDREN, 0]
-                    side = sides[mine, jnp.maximum(n, 0)]
-                    left.append(jnp.concatenate([side[:, : 2 * RANK], side], axis=1))
-                    live.append(n >= 0)
-                schur = matmul(jnp.concatenate(left, axis=0), right)
                 column = pl.multiple_of((other % CHILDREN) * RANK, RANK)
-                row = other // CHILDREN - low
-                for mine in range(per_device):
-                    apart = other - number - mine
-                    value = jnp.where(live[mine], schur[mine * RANK : (mine + 1) * RANK], 0.0)
-
-                    @pl.when((apart <= REACH) & (apart >= -REACH))
-                    def _(mine=mine, value=value):
+                yield holder, leaf, slot_of(delta, holder), other, other // CHILDREN - low, column
+
+    def keep(turn, values):
+        for (other, row, column, mine), act in values:
+            if turn in (3, 4):
+                apart = other - number - mine
+                pl.when((apart <= REACH) & (apart >= -REACH))(lambda: act(row, column, mine))
+            else:
+                act(row, column, mine)
+
+    def first_half(turn):
+        for leaf in range(per_device):
+            relayed(0, deltas[turn], leaf).wait_recv()
+        coupled = {}
+        targets_of = {}
+        for holder, leaf, slot, other, row, column in pairs_of(turn):
+            left = []
+            for mine in range(per_device):
+                n = lookup[mine, other - number - mine + reach // 2, 0]
+                left.append(halves[mine, n])
+                targets_of[holder, leaf, mine] = (other, row, column, mine)
+            both = matmul(jnp.concatenate(left, axis=0), win_bases[slot, leaf])
+            for mine in range(per_device):
+                part = both[mine * 2 * RANK : (mine + 1) * 2 * RANK]
+                high, low_part = split(part[red:, :red])
+                here_rows = pl.ds(mine * RANK, RANK)
+                lefts[turn, holder, leaf, here_rows, :red] = high
+                lefts[turn, holder, leaf, here_rows, red:] = low_part
+                coupled[holder, leaf, mine] = (split(part[:red, red:]), part[red:, red:])
+        kept = []
+        for holder in range(2):
+            for mine in range(per_device):
+                tall = [
+                    jnp.concatenate(coupled[holder, leaf, mine][0], axis=0)
+                    for leaf in range(per_device)
+                ]
+                moved = matmul(turned[mine], jnp.concatenate(tall, axis=1))
+                for leaf in range(per_device):
+                    value = coupled[holder, leaf, mine][1] + moved[:, leaf * RANK : (leaf + 1) * RANK]
+
+                    def act(row, column, mine, value=value):
                         blocks[mine, row, :, pl.ds(column, RANK)] = value
+
+                    kept.append((targets_of[holder, leaf, mine], act))
+        keep(turn, kept)
+
+    def second_half(turn):
+        for leaf in range(per_device):
+            relayed(1, deltas[turn], leaf).wait_recv()
+        kept = []
+        for holder, leaf, slot, other, row, column in pairs_of(turn):
+            moved = win_shift[slot, leaf]
+            both = matmul(lefts[turn, holder, leaf], jnp.concatenate([moved, moved], axis=0))
+            for mine in range(per_device):
+                value = both[mine * RANK : (mine + 1) * RANK]
+
+                def act(row, column, mine, value=value):
+                    spot = blocks[mine, row, :, pl.ds(column, RANK)]
+                    blocks[mine, row, :, pl.ds(column, RANK)] = spot - value
+
+                kept.append(((other, row, column, mine), act))
+        keep(turn, kept)
+
+    def run(half, turn):
+        pl.when(exists(deltas[turn]))(lambda: half(turn))
 
     def row_copy(t):
         other = (seat + t) % size
@@ -456,25 +508,46 @@
             device_id_type=MESH,
         )
 
-    served = 0
-    chunks = len(orders[0][0])
-    for turn in range(chunks):
-        if turn:
-            needed = max(order[1][turn - 1] for order in orders)
-            while served < needed:
-                served += 1
-                serve(1, served)
-        delta = pick([order[0][turn] for order in orders])
-        pl.when(exists(delta))(lambda: couple(delta))
-        if turn == 0:
-            for leaf in range(per_device):
-                column = pl.multiple_of(((number + leaf) % CHILDREN) * RANK, RANK)
-                blocks[leaf, home, :, pl.ds(column, RANK)] = skeleton[leaf]
-        if turn == 1:
-            for leaf in range(per_device):
-                diagonal[leaf] = blocks[leaf, home].astype(jnp.bfloat16)
-            for t in range(1, size):
-                row_copy(t).start()
+    served = [red // PANEL - 2, 0]
+
+    def serve_to(kind, step):
+        while served[kind] < step:
+            served[kind] += 1
+            serve(kind, served[kind])
+
+    for copy in fetches:
+        copy.wait()
+    table.wait()
+    for turn in range(slots // unroll):
+        project(turn)
+        serve_to(0, red // PANEL - 1 + turn)
+    finish_factor(factor, panel, skeleton, rows, low_corner)
+    near_chunks = [turn for turn in range(chunks) if steps[turn] <= 2]
+    far_chunks = [turn for turn in range(chunks) if steps[turn] > 2]
+    for turn in near_chunks[:2]:
+        run(first_half, turn)
+    serve_to(1, 2)
+    for turn in near_chunks[:2]:
+        run(second_half, turn)
+    for leaf in range(per_device):
+        column = pl.multiple_of(((number + leaf) % CHILDREN) * RANK, RANK)
+        blocks[leaf, home, :, pl.ds(column, RANK)] = skeleton[leaf]
+    for leaf in range(per_device):
+        diagonal[leaf] = blocks[leaf, home].astype(jnp.bfloat16)
+    for t in range(1, size):
+        row_copy(t).start()
+    for turn in near_chunks[2:]:
+        run(first_half, turn)
+    serve_to(0, STEPS)
+    for turn in near_chunks[2:]:
+        run(second_half, turn)
+    serve_to(1, 3)
+    for turn in far_chunks:
+        run(first_half, turn)
+    for turn in far_chunks:
+        serve_to(1, steps[turn])
+        run(second_half, turn)
+    serve_to(1, STEPS)
 
     finish(0)
     finish(1)
@@ -548,24 +621,28 @@
             out((per_device, targets, RANK, CHILDREN * RANK), f32),
             out((size, per_device, RANK, width), bf16),
         ),
-        in_specs=[vmem, vmem, vmem, hbm],
+        in_specs=[hbm] * 4,
         out_specs=(vmem,) * 4,
         scratch_shapes=[
             pltpu.VMEM((window,) + bases.shape, bf16),
             pltpu.VMEM((window, per_device, red, RANK), bf16),
-            pltpu.VMEM((per_device, red, RANK), bf16),
+            pltpu.VMEM(diag_blocks.shape, bf16),
+            pltpu.VMEM(leaf_nbrs.shape, jnp.int32),
             pltpu.VMEM((per_device, RANK, RANK), f32),
+            pltpu.VMEM((per_device, RANK, RANK), f32),
+            pltpu.VMEM((per_device, RANK, 2 * red), bf16),
             pltpu.VMEM(bases.shape, bf16),
             pltpu.VMEM((per_device, red, 2 * red + RANK), f32),
             pltpu.VMEM((per_device, red, 2 * red + RANK), f32),
             pltpu.VMEM(near_blocks.shape, bf16),
-            pltpu.VMEM((per_device, slots, RANK, 6 * RANK), bf16),
+            pltpu.VMEM((per_device, slots + 1) + near_blocks.shape[2:], bf16),
+            pltpu.VMEM((2 * PLANE + 1, 2, per_device, per_device * RANK, 2 * red), bf16),
             pltpu.VMEM((per_device, RANK, CHILDREN * RANK), bf16),
             sems((2, len(LINKS), links)),
             sems((2, 2 * PLANE + 1, per_device)),
             sems((2, 2 * PLANE + 1, per_device)),
             sems((2, 2 * PLANE + 1, per_device)),
-            sems((2,)),
+            sems((3,)),
             sems((per_device,)),
             sems((size,)),
             sems((size,)),

time: 63 us -> 46.3 us (0.73)
  the two profiles are of different devices: /device:TPU:7 before, /device:TPU:5 now
where the time goes in v2:
time: 46.3 us; the launch traced here: 46.1 us
  Pallas kernels  42.7 us (92%)
  local copies, waits for them, and re-layouts  2.57 us (6%)
  between operations  0.82 us (2%)
    pallas_call x1, Pallas kernels, local(): pl.pallas_call(functools.partial(level_kernel, count, parents, targets),...  39.2 us
    pallas_call x1, Pallas kernels, local(): pl.pallas_call(place_kernel, out_shape=(out((per_device, red, red), f32),...  3.49 us
    unnamed x8, local copies, waits for them, and re-layouts  2.57 us

profile of v2, /device:TPU:5, one launch (start us, length us, event | category | flops | bytes accessed | tf_op | source)
XLA Modules:
  0.0 46.1 jit_solution(16206758289136540396)
XLA Ops:
  0.6 0.0 copy-start
  0.6 0.9 %copy-done = bf16[2,256,256]{2,1,0:T(8,128)(2,1)S(1)} copy-done((bf16[2,256,256]{2,1,0:T(8,128)(2,1)S(1)}, bf16[2,256,256]{2,1,0:T(8,128)(2,1)}, u32[]{:S(2)}) %copy-start) | copy-done | bytes 262168
  1.6 0.0 copy-start.1
  1.6 0.9 %copy-done.1 = bf16[2,256,256]{2,1,0:T(8,128)(2,1)S(1)} copy-done((bf16[2,256,256]{2,1,0:T(8,128)(2,1)S(1)}, bf16[2,256,256]{2,1,0:T(8,128)(2,1)}, u32[]{:S(2)}) %copy-start.1) | copy-done | bytes 262168
  2.5 0.0 copy-start.3
  2.5 0.7 %copy-done.3 = s32[2,26]{1,0:T(2,128)S(1)} copy-done((s32[2,26]{1,0:T(2,128)S(1)}, s32[2,26]{1,0:T(2,128)}, u32[]{:S(2)}) %copy-start.3) | copy-done | bytes 232
  3.2 0.0 copy-start.2
  3.2 39.2 %level.1 = (f32[2,128,128]{2,1,0:T(8,128)S(1)}, f32[2,128,128]{2,1,0:T(8,128)S(1)}, f32[2,5,128,1024]{3,2,1,0:T(8,128)S(1)}, bf16[4,2,128,256]{3,2,1,0:T(8,128)(2,1)S(1)}) custom-call(s32[2,26]{1,0:T(2,128)S(1)} %copy-done.3, bf16[2,256,256]{2,1,0:T(8,128)(2,1)S(1)} %copy-done, bf16[2,256,256]{2,1,0:T(8,128)(2,1)S(1)} %copy-done.1, ...), custom_call_target="tpu_custom_call" | custom-call | tf_op jit(solution)/shard_map/level/pallas_call | solution.py:616
  42.5 0.0 copy-done.2
  42.5 3.5 %place.1 = (f32[2,128,128]{2,1,0:T(8,128)}, f32[2,128,128]{2,1,0:T(8,128)}, f32[2,5,128,1024]{3,2,1,0:T(8,128)}, f32[256,1024]{1,0:T(8,128)}) custom-call(s32[8,5]{1,0:T(8,128)S(1)} %copy-done.2, f32[2,128,128]{2,1,0:T(8,128)S(1)} %get-tuple-element.8.factor, f32[2,128,128]{2,1,0:T(8,128)S(1)} %get-tuple-element.9.panel, ...), custom_call_target="tpu_custom_call" | custom-call | tf_op jit(solution)/shard_map/place/pallas_call | solution.py:659
Async XLA Ops:
  0.6 1.0 %copy-start = (bf16[2,256,256]{2,1,0:T(8,128)(2,1)S(1)}, bf16[2,256,256]{2,1,0:T(8,128)(2,1)}, u32[]{:S(2)}) copy-start(bf16[2,256,256]{2,1,0:T(8,128)(2,1)} %diag.1) | copy-start | bytes 786436
  1.6 0.9 %copy-start.1 = (bf16[2,256,256]{2,1,0:T(8,128)(2,1)S(1)}, bf16[2,256,256]{2,1,0:T(8,128)(2,1)}, u32[]{:S(2)}) copy-start(bf16[2,256,256]{2,1,0:T(8,128)(2,1)} %bases.1) | copy-start | bytes 786436
  2.5 0.7 %copy-start.3 = (s32[2,26]{1,0:T(2,128)S(1)}, s32[2,26]{1,0:T(2,128)}, u32[]{:S(2)}) copy-start(s32[2,26]{1,0:T(2,128)} %nbrs.1) | copy-start | bytes 628
  3.2 39.3 %copy-start.2 = (s32[8,5]{1,0:T(8,128)S(1)}, s32[8,5]{1,0:T(8,128)}, u32[]{:S(2)}) copy-start(s32[8,5]{1,0:T(8,128)} %parents.1) | copy-start | bytes 484

commit v3 on v2

--- a/solution.py
+++ b/solution.py
@@ -27,43 +27,76 @@
     )
 
 
-def plan():
-    def both(plane, chip):
-        return [(plane, chip, 0), (plane, chip, 1)]
-
-    inbound = (
-        {
-            "x": both(0, 1) + [(0, 3, 0), (-1, 1, 0)],
-            "y": both(0, 2) + [(0, 3, 1)] + both(-1, 2),
-            "up": both(-1, 0) + [(-1, 1, 1)] + both(-1, 3),
-            "down": both(1, 0),
-        },
-        {
-            "x": both(0, 0) + both(0, 2),
-            "y": both(0, 3) + both(-1, 3),
-            "up": both(-1, 1) + both(-1, 2),
-            "down": both(1, 1) + both(1, 0),
-        },
-        {
-            "x": both(0, 3) + both(0, 1),
-            "y": both(0, 0) + both(1, 0),
-            "up": both(-1, 2) + both(-1, 3),
-            "down": both(1, 2) + both(1, 1),
-        },
-        {
-            "x": both(0, 2) + [(0, 0, 0), (1, 2, 0)],
-            "y": both(0, 1) + [(0, 0, 1)] + both(1, 1),
-            "up": both(-1, 3),
-            "down": both(1, 3) + [(1, 2, 1)] + both(1, 0),
-        },
-    )
+def halves_of(plane, chip):
+    return [(plane, chip, 0), (plane, chip, 1)]
+
+
+def whole(plane, chip):
+    return [(plane, chip, None)]
+
+
+BASES_IN = (
+    {
+        "x": halves_of(0, 1) + [(0, 3, 0), (-1, 1, 0)],
+        "y": halves_of(0, 2) + [(0, 3, 1)] + halves_of(-1, 2),
+        "up": halves_of(-1, 0) + [(-1, 1, 1)] + halves_of(-1, 3),
+        "down": halves_of(1, 0),
+    },
+    {
+        "x": halves_of(0, 0) + halves_of(0, 2),
+        "y": halves_of(0, 3) + halves_of(-1, 3),
+        "up": halves_of(-1, 1) + halves_of(-1, 2),
+        "down": halves_of(1, 1) + halves_of(1, 0),
+    },
+    {
+        "x": halves_of(0, 3) + halves_of(0, 1),
+        "y": halves_of(0, 0) + halves_of(1, 0),
+        "up": halves_of(-1, 2) + halves_of(-1, 3),
+        "down": halves_of(1, 2) + halves_of(1, 1),
+    },
+    {
+        "x": halves_of(0, 2) + [(0, 0, 0), (1, 2, 0)],
+        "y": halves_of(0, 1) + [(0, 0, 1)] + halves_of(1, 1),
+        "up": halves_of(-1, 3),
+        "down": halves_of(1, 3) + [(1, 2, 1)] + halves_of(1, 0),
+    },
+)
+SHIFTS_IN = (
+    {
+        "x": whole(0, 1) + whole(-1, 1),
+        "y": whole(0, 2) + whole(0, 3) + whole(-1, 2),
+        "up": whole(-1, 0) + whole(-1, 3),
+        "down": whole(1, 0),
+    },
+    {
+        "x": whole(0, 0) + whole(0, 2),
+        "y": whole(0, 3) + whole(-1, 3),
+        "up": whole(-1, 1) + whole(-1, 2),
+        "down": whole(1, 1) + whole(1, 0),
+    },
+    {
+        "x": whole(0, 3) + whole(0, 1),
+        "y": whole(0, 0) + whole(1, 0),
+        "up": whole(-1, 2) + whole(-1, 3),
+        "down": whole(1, 2) + whole(1, 1),
+    },
+    {
+        "x": whole(0, 2) + whole(1, 2),
+        "y": whole(0, 1) + whole(0, 0) + whole(1, 1),
+        "up": whole(-1, 3),
+        "down": whole(1, 3) + whole(1, 0),
+    },
+)
+
+
+def plan(inbound):
     outbound = []
     for place in range(PLANE):
         out = {"x": inbound[place ^ 1]["x"], "y": inbound[place ^ 2]["y"]}
         out["up"] = [(plane + 1, chip, leaf) for plane, chip, leaf in inbound[place]["up"]]
         out["down"] = [(plane - 1, chip, leaf) for plane, chip, leaf in inbound[place]["down"]]
         outbound.append(out)
-    held = [{(0, place, leaf): 0 for leaf in range(2)} for place in range(PLANE)]
+    held = [{(0, place, leaf): 0 for leaf in (0, 1, None)} for place in range(PLANE)]
     arrivals = [[] for _ in range(PLANE)]
     queue = {(place, link): 0 for place in range(PLANE) for link in LINKS}
     now = 0
@@ -79,11 +112,10 @@
         for target, item in landed:
             held[target][item] = now
             arrivals[target].append((now, item))
-    return outbound, arrivals
-
-
-OUTBOUND, ARRIVALS = plan()
-STEPS = max(now for events in ARRIVALS for now, _ in events)
+    return outbound, arrivals, now
+
+
+OUTBOUND, ARRIVALS, STEPS = zip(plan(BASES_IN), plan(SHIFTS_IN))
 
 
 def shift_of(place, item):
@@ -92,13 +124,14 @@
 
 
 def chunk_order(place):
-    ready = {0: 0}
-    for now, item in ARRIVALS[place]:
-        ready[shift_of(place, item)] = now
+    ready = [{0: 0}, {0: 0}]
+    for kind in range(2):
+        for now, item in ARRIVALS[kind][place]:
+            ready[kind][shift_of(place, item)] = now
     first = [0, (place ^ 1) - place, (place ^ 2) - place, -PLANE, PLANE]
-    rest = sorted((now, delta) for delta, now in ready.items() if delta not in first)
-    order = first + [delta for _, delta in rest]
-    return order, [ready[delta] for delta in order]
+    rest = sorted((ready[1][delta], now, delta) for delta, now in ready[0].items() if delta not in first)
+    order = first + [delta for _, _, delta in rest]
+    return order, [(ready[0][delta], ready[1][delta]) for delta in order]
 
 
 def reduce_blocks(diag, bases, bases_t, work, low_corner):
@@ -257,60 +290,62 @@
     def slot_of(delta, holder):
         return 2 * (PLANE + delta) + holder
 
+    def block_of(kind, delta, holder, leaf):
+        block = windows[kind].at[slot_of(delta, holder)]
+        return block if leaf is None else block.at[leaf]
+
     def hop(kind, at, link, order):
-        item = OUTBOUND[at][link][order]
-        delta = shift_of(at, item)
+        item = OUTBOUND[kind][at][link][order]
+        delta, leaf = shift_of(at, item), item[2]
         moved = {"x": at - (at ^ 1), "y": at - (at ^ 2), "up": -PLANE, "down": PLANE}[link]
-        window = windows[kind]
-        leaf = item[2]
         return pltpu.make_async_remote_copy(
-            src_ref=window.at[slot_of(delta, core), leaf],
-            dst_ref=window.at[slot_of(delta + moved, core), leaf],
+            src_ref=block_of(kind, delta, core, leaf),
+            dst_ref=block_of(kind, delta + moved, core, leaf),
             send_sem=send.at[kind, LINKS.index(link), order],
-            recv_sem=recv.at[kind, PLANE + delta + moved, leaf],
+            recv_sem=recv.at[kind, PLANE + delta + moved, leaf or 0],
             device_id=(device[link],),
             device_id_type=MESH,
         )
 
     def arrival(kind, delta, leaf):
-        window = windows[kind]
-        there = window.at[slot_of(delta, core), leaf]
+        there = block_of(kind, delta, core, leaf)
         return pltpu.make_async_remote_copy(
             src_ref=there,
             dst_ref=there,
             send_sem=send.at[kind, 0, 0],
-            recv_sem=recv.at[kind, PLANE + delta, leaf],
+            recv_sem=recv.at[kind, PLANE + delta, leaf or 0],
             device_id=(sibling,),
             device_id_type=MESH,
         )
 
     def relay(kind, delta, leaf):
-        window = windows[kind]
-        there = window.at[slot_of(delta, core), leaf]
+        there = block_of(kind, delta, core, leaf)
         return pltpu.make_async_remote_copy(
             src_ref=there,
             dst_ref=there,
-            send_sem=pass_send.at[kind, PLANE + delta, leaf],
-            recv_sem=pass_recv.at[kind, PLANE + delta, leaf],
+            send_sem=pass_send.at[kind, PLANE + delta, leaf or 0],
+            recv_sem=pass_recv.at[kind, PLANE + delta, leaf or 0],
             device_id=(sibling,),
             device_id_type=MESH,
         )
 
     def relayed(kind, delta, leaf):
-        window = windows[kind]
-        there = window.at[slot_of(delta, 1 - core), leaf]
+        there = block_of(kind, delta, 1 - core, leaf)
         return pltpu.make_async_remote_copy(
             src_ref=there,
             dst_ref=there,
-            send_sem=pass_send.at[kind, PLANE + delta, leaf],
-            recv_sem=pass_recv.at[kind, PLANE + delta, leaf],
+            send_sem=pass_send.at[kind, PLANE + delta, leaf or 0],
+            recv_sem=pass_recv.at[kind, PLANE + delta, leaf or 0],
             device_id=(sibling,),
             device_id_type=MESH,
         )
 
+    def parts(kind):
+        return (None,) if kind else range(per_device)
+
     def on_links(kind, at, item, act):
         for link in LINKS:
-            for order, entry in enumerate(OUTBOUND[at][link]):
+            for order, entry in enumerate(OUTBOUND[kind][at][link]):
                 if entry == item:
                     if link in present:
                         pl.when(present[link])(lambda: act(hop(kind, at, link, order)))
@@ -329,16 +364,16 @@
 
     def dispatch(kind):
         def act(at):
-            for leaf in range(per_device):
+            for leaf in parts(kind):
                 on_links(kind, at, (0, at, leaf), start)
 
         by_place(act)
-        for leaf in range(per_device):
+        for leaf in parts(kind):
             relay(kind, 0, leaf).start()
 
     def serve(kind, step):
         def act(at):
-            for now, item in ARRIVALS[at]:
+            for now, item in ARRIVALS[kind][at]:
                 if now == step:
                     delta, leaf = shift_of(at, item), item[2]
 
@@ -356,9 +391,9 @@
 
     def finish(kind):
         def act(at):
-            for leaf in range(per_device):
+            for leaf in parts(kind):
                 on_links(kind, at, (0, at, leaf), stop)
-            for _, item in ARRIVALS[at]:
+            for _, item in ARRIVALS[kind][at]:
                 delta, leaf = shift_of(at, item), item[2]
 
                 def one():
@@ -371,7 +406,7 @@
                     pl.when(exists(delta))(one)
 
         by_place(act)
-        for leaf in range(per_device):
+        for leaf in parts(kind):
             relay(kind, 0, leaf).wait_send()
 
     number = me * per_device
@@ -422,7 +457,6 @@
         return chosen
 
     deltas = [pick([order[0][turn] for order in orders]) for turn in range(chunks)]
-    steps = [max(order[1][turn] for order in orders) for turn in range(chunks)]
 
     def pairs_of(turn):
         delta = deltas[turn]
@@ -441,7 +475,7 @@
                 act(row, column, mine)
 
     def first_half(turn):
-        for leaf in range(per_device):
+        for leaf in parts(0):
             relayed(0, deltas[turn], leaf).wait_recv()
         coupled = {}
         targets_of = {}
@@ -477,7 +511,7 @@
         keep(turn, kept)
 
     def second_half(turn):
-        for leaf in range(per_device):
+        for leaf in parts(1):
             relayed(1, deltas[turn], leaf).wait_recv()
         kept = []
         for holder, leaf, slot, other, row, column in pairs_of(turn):
@@ -508,27 +542,19 @@
             device_id_type=MESH,
         )
 
-    served = [red // PANEL - 2, 0]
-
-    def serve_to(kind, step):
-        while served[kind] < step:
-            served[kind] += 1
-            serve(kind, served[kind])
-
+    serve(0, 3)
     for copy in fetches:
         copy.wait()
     table.wait()
     for turn in range(slots // unroll):
         project(turn)
-        serve_to(0, red // PANEL - 1 + turn)
+    for turn in range(2):
+        run(first_half, turn)
+    serve(1, 1)
+    serve(0, 4)
+    for turn in range(2):
+        run(second_half, turn)
     finish_factor(factor, panel, skeleton, rows, low_corner)
-    near_chunks = [turn for turn in range(chunks) if steps[turn] <= 2]
-    far_chunks = [turn for turn in range(chunks) if steps[turn] > 2]
-    for turn in near_chunks[:2]:
-        run(first_half, turn)
-    serve_to(1, 2)
-    for turn in near_chunks[:2]:
-        run(second_half, turn)
     for leaf in range(per_device):
         column = pl.multiple_of(((number + leaf) % CHILDREN) * RANK, RANK)
         blocks[leaf, home, :, pl.ds(column, RANK)] = skeleton[leaf]
@@ -536,18 +562,19 @@
         diagonal[leaf] = blocks[leaf, home].astype(jnp.bfloat16)
     for t in range(1, size):
         row_copy(t).start()
-    for turn in near_chunks[2:]:
+    for turn in range(2, 5):
         run(first_half, turn)
-    serve_to(0, STEPS)
-    for turn in near_chunks[2:]:
+    serve(1, 2)
+    for turn in range(2, 5):
         run(second_half, turn)
-    serve_to(1, 3)
-    for turn in far_chunks:
+    for step in range(5, STEPS[0] + 1):
+        serve(0, step)
+    for turn in range(5, chunks):
         run(first_half, turn)
-    for turn in far_chunks:
-        serve_to(1, steps[turn])
+    for step in range(3, STEPS[1] + 1):
+        serve(1, step)
+    for turn in range(5, chunks):
         run(second_half, turn)
-    serve_to(1, STEPS)
 
     finish(0)
     finish(1)
@@ -604,6 +631,9 @@
     hbm = pl.BlockSpec(memory_space=pltpu.HBM)
     f32, bf16 = jnp.float32, jnp.bfloat16
 
+    def in_hbm(array):
+        return pltpu.with_memory_space_constraint(array, pltpu.HBM)
+
     def out(shape, dtype):
         return jax.ShapeDtypeStruct(shape, dtype)
 
@@ -611,7 +641,7 @@
     size = CHILDREN // per_device
     width = per_device * RANK
     window = 2 * (2 * PLANE + 1)
-    links = max(len(out_[link]) for out_ in OUTBOUND for link in LINKS)
+    links = max(len(out_[link]) for kind in OUTBOUND for out_ in kind for link in LINKS)
     sems = pltpu.SemaphoreType.DMA
     factor, panel, blocks, landed = pl.pallas_call(
         functools.partial(level_kernel, count, parents, targets),
@@ -654,7 +684,7 @@
             collective_id=0, has_side_effects=True, vmem_limit_bytes=46_500_000
         ),
         name="level",
-    )(leaf_nbrs, diag_blocks, bases, near_blocks)
+    )(*(in_hbm(array) for array in (leaf_nbrs, diag_blocks, bases, near_blocks)))
 
     return pl.pallas_call(
         place_kernel,

time: 46.3 us -> 41.1 us (0.89)
  the two profiles are of different devices: /device:TPU:5 before, /device:TPU:17 now
where the time goes in v3:
time: 41.1 us; the launch traced here: 40.9 us
  Pallas kernels  40.1 us (98%)
  between operations  0.82 us (2%)
    pallas_call x1, Pallas kernels, local(): pl.pallas_call(functools.partial(level_kernel, count, parents, targets),...  36.6 us
    pallas_call x1, Pallas kernels, local(): pl.pallas_call(place_kernel, out_shape=(out((per_device, red, red), f32),...  3.49 us

profile of v3, /device:TPU:17, one launch (start us, length us, event | category | flops | bytes accessed | tf_op | source)
XLA Modules:
  0.0 40.9 jit_solution(12459528899930056125)
XLA Ops:
  0.6 0.0 copy-start
  0.6 36.6 %level.1 = (f32[2,128,128]{2,1,0:T(8,128)S(1)}, f32[2,128,128]{2,1,0:T(8,128)S(1)}, f32[2,5,128,1024]{3,2,1,0:T(8,128)S(1)}, bf16[4,2,128,256]{3,2,1,0:T(8,128)(2,1)S(1)}) custom-call(s32[2,26]{1,0:T(2,128)} %nbrs.1, bf16[2,256,256]{2,1,0:T(8,128)(2,1)} %diag.1, bf16[2,256,256]{2,1,0:T(8,128)(2,1)} %bases.1, bf16[2,26,256,256]{3,2,1,0:T(8,128)(2,1)} %near.1), custom_call_target="tpu_custom_call" | custom-call | tf_op jit(solution)/shard_map/level/pallas_call | solution.py:646
  37.2 0.0 copy-done
  37.2 3.5 %place.1 = (f32[2,128,128]{2,1,0:T(8,128)}, f32[2,128,128]{2,1,0:T(8,128)}, f32[2,5,128,1024]{3,2,1,0:T(8,128)}, f32[256,1024]{1,0:T(8,128)}) custom-call(s32[8,5]{1,0:T(8,128)S(1)} %copy-done, f32[2,128,128]{2,1,0:T(8,128)S(1)} %get-tuple-element.8.factor, f32[2,128,128]{2,1,0:T(8,128)S(1)} %get-tuple-element.9.panel, ...), custom_call_target="tpu_custom_call" | custom-call | tf_op jit(solution)/shard_map/place/pallas_call | solution.py:689
Async XLA Ops:
  0.6 36.6 %copy-start = (s32[8,5]{1,0:T(8,128)S(1)}, s32[8,5]{1,0:T(8,128)}, u32[]{:S(2)}) copy-start(s32[8,5]{1,0:T(8,128)} %parents.1) | copy-start | bytes 484

commit v4 on v3

--- a/solution.py
+++ b/solution.py
@@ -11,6 +11,8 @@
 REACH = 16
 CHILDREN = 8
 PANEL = 32
+GROUP = 8
+LANES = 128
 PLANE = 4
 LINKS = ("x", "y", "up", "down")
 MESH = pl.DeviceIdType.MESH
@@ -154,26 +156,60 @@
 
 def eliminate(shift, turned, work, rows, serve):
     per_device, red = work.shape[0], work.shape[1]
-    wide = 2 * red + RANK
+    tiles = work.shape[2] // LANES
     row_id = lax.broadcasted_iota(jnp.int32, (red, red), 0)
     col_id = lax.broadcasted_iota(jnp.int32, (red, red), 1)
-    sub = lax.broadcasted_iota(jnp.int32, (PANEL, 1), 0)
+    sub = lax.broadcasted_iota(jnp.int32, (GROUP, LANES), 0)
+    groups = PANEL // GROUP
+    leaves = range(per_device)
     for start in range(0, red, PANEL):
-        strips = [work[leaf, start : start + PANEL, :] for leaf in range(per_device)]
-        for k in range(PANEL):
-            for leaf in range(per_device):
-                strip = strips[leaf]
-                column = strip[:, start + k : start + k + 1]
-                ratio = jnp.where(sub > k, column / column[k : k + 1], 0.0)
-                strips[leaf] = strip - ratio * strip[k : k + 1, :]
-        lane = lax.broadcasted_iota(jnp.int32, (PANEL, wide), 1)
-        line = lax.broadcasted_iota(jnp.int32, (PANEL, wide), 0)
-        for leaf in range(per_device):
-            strip = strips[leaf]
-            pivots = jnp.sum(jnp.where(lane == line + start, strip, 0.0), axis=1, keepdims=True)
-            strip = strip * (1.0 / jnp.sqrt(pivots))
-            rows[leaf, start : start + PANEL, :] = strip
-            if start + PANEL < red:
+        strips = [
+            [
+                [
+                    work[leaf, pl.ds(start + GROUP * v, GROUP), pl.ds(LANES * t, LANES)]
+                    for t in range(tiles)
+                ]
+                for v in range(groups)
+            ]
+            for leaf in leaves
+        ]
+        for g in range(groups):
+            first = start + GROUP * g
+            columns = [
+                {
+                    v: [
+                        jnp.broadcast_to(strips[leaf][v][0][:, first + c : first + c + 1], (GROUP, LANES))
+                        for c in range(GROUP)
+                    ]
+                    for v in range(g, groups)
+                }
+                for leaf in leaves
+            ]
+            for r in range(GROUP):
+                for leaf in leaves:
+                    cols, strip = columns[leaf], strips[leaf]
+                    inverse = 1.0 / cols[g][r][r : r + 1]
+                    heads = [cols[g][c][r : r + 1] for c in range(GROUP)]
+                    lines = [strip[g][t][r : r + 1] for t in range(tiles)]
+                    for v in range(g, groups):
+                        ratio = cols[v][r] * inverse
+                        if v == g:
+                            ratio = jnp.where(sub > r, ratio, 0.0)
+                        for c in range(r + 1, GROUP):
+                            cols[v][c] = cols[v][c] - ratio * heads[c]
+                        for t in range(tiles):
+                            strip[v][t] = strip[v][t] - ratio * lines[t]
+            for leaf in leaves:
+                pivots = columns[leaf][g][0]
+                for r in range(1, GROUP):
+                    pivots = jnp.where(sub == r, columns[leaf][g][r], pivots)
+                scale = 1.0 / jnp.sqrt(pivots)
+                for t in range(tiles):
+                    here = (leaf, pl.ds(first, GROUP), pl.ds(LANES * t, LANES))
+                    rows[here] = strips[leaf][g][t] * scale
+        if start + PANEL < red:
+            for leaf in leaves:
+                strip = rows[leaf, start : start + PANEL, :]
                 work[leaf] = work[leaf] - matmul_t(strip[:, :red], strip, highest)
         serve(start // PANEL)
     for leaf in range(per_device):
@@ -413,6 +449,18 @@
     parent = number // CHILDREN
     low = jnp.clip(parent - targets // 2, 0, parents - targets)
     home = parent - low
+    inputs[1].wait()
+    pl.semaphore_wait(barrier, peers)
+    dispatch(0)
+    inputs[2].wait()
+    reduce_blocks(diag_in, win_bases.at[here], bases_t, work, low_corner)
+
+    def between(panel_done):
+        if panel_done > 0 and panel_done < red // PANEL - 1:
+            serve(0, panel_done)
+
+    eliminate(win_shift.at[here], turned, work, rows, between)
+    dispatch(1)
     blocks[...] = jnp.zeros_like(blocks)
     halves[:, slots] = jnp.zeros_like(halves[:, slots])
     reach = found.shape[1]
@@ -426,18 +474,6 @@
         found[leaf] = jnp.broadcast_to(jnp.where(slot < 0, slots, slot), found.shape[1:])
     table = pltpu.make_async_copy(found, lookup, found_sem)
     table.start()
-    for copy in inputs[1:]:
-        copy.wait()
-    reduce_blocks(diag_in, win_bases.at[here], bases_t, work, low_corner)
-    pl.semaphore_wait(barrier, peers)
-    dispatch(0)
-
-    def between(panel_done):
-        if panel_done > 0 and panel_done < red // PANEL - 1:
-            serve(0, panel_done)
-
-    eliminate(win_shift.at[here], turned, work, rows, between)
-    dispatch(1)
 
     unroll = max(n for n in range(1, 14) if slots % n == 0)
 

time: 41.1 us -> 39 us (0.949)
  Pallas kernels: 40.1 us -> 38 us
    pallas_call x1, Pallas kernels: 36.6 us -> 34.5 us  [local(): pl.pallas_call(functools.partial(level_kernel, count, parents, targets),...]
where the time goes in v4:
time: 39 us; the launch traced here: 38.8 us
  Pallas kernels  38 us (97%)
  between operations  0.82 us (2%)
    pallas_call x1, Pallas kernels, local(): pl.pallas_call(functools.partial(level_kernel, count, parents, targets),...  34.5 us
    pallas_call x1, Pallas kernels, local(): pl.pallas_call(place_kernel, out_shape=(out((per_device, red, red), f32),...  3.49 us

profile of v4, /device:TPU:17, one launch (start us, length us, event | category | flops | bytes accessed | tf_op | source)
XLA Modules:
  0.0 38.8 jit_solution(17181567112891175094)
XLA Ops:
  0.6 0.0 copy-start
  0.6 34.5 %level.1 = (f32[2,128,128]{2,1,0:T(8,128)S(1)}, f32[2,128,128]{2,1,0:T(8,128)S(1)}, f32[2,5,128,1024]{3,2,1,0:T(8,128)S(1)}, bf16[4,2,128,256]{3,2,1,0:T(8,128)(2,1)S(1)}) custom-call(s32[2,26]{1,0:T(2,128)} %nbrs.1, bf16[2,256,256]{2,1,0:T(8,128)(2,1)} %diag.1, bf16[2,256,256]{2,1,0:T(8,128)(2,1)} %bases.1, bf16[2,26,256,256]{3,2,1,0:T(8,128)(2,1)} %near.1), custom_call_target="tpu_custom_call" | custom-call | tf_op jit(solution)/shard_map/level/pallas_call | solution.py:682
  35.1 0.0 copy-done
  35.2 3.5 %place.1 = (f32[2,128,128]{2,1,0:T(8,128)}, f32[2,128,128]{2,1,0:T(8,128)}, f32[2,5,128,1024]{3,2,1,0:T(8,128)}, f32[256,1024]{1,0:T(8,128)}) custom-call(s32[8,5]{1,0:T(8,128)S(1)} %copy-done, f32[2,128,128]{2,1,0:T(8,128)S(1)} %get-tuple-element.8.factor, f32[2,128,128]{2,1,0:T(8,128)S(1)} %get-tuple-element.9.panel, ...), custom_call_target="tpu_custom_call" | custom-call | tf_op jit(solution)/shard_map/place/pallas_call | solution.py:725
Async XLA Ops:
  0.6 34.5 %copy-start = (s32[8,5]{1,0:T(8,128)S(1)}, s32[8,5]{1,0:T(8,128)}, u32[]{:S(2)}) copy-start(s32[8,5]{1,0:T(8,128)} %parents.1) | copy-start | bytes 484

commit v5 on v4

--- a/solution.py
+++ b/solution.py
@@ -45,16 +45,16 @@
         "down": halves_of(1, 0),
     },
     {
-        "x": halves_of(0, 0) + halves_of(0, 2),
-        "y": halves_of(0, 3) + halves_of(-1, 3),
-        "up": halves_of(-1, 1) + halves_of(-1, 2),
+        "x": halves_of(0, 0) + [(0, 2, 0)],
+        "y": halves_of(0, 3) + [(0, 2, 1), (-1, 3, 0)],
+        "up": halves_of(-1, 1) + [(-1, 3, 1)] + halves_of(-1, 2),
         "down": halves_of(1, 1) + halves_of(1, 0),
     },
     {
-        "x": halves_of(0, 3) + halves_of(0, 1),
-        "y": halves_of(0, 0) + halves_of(1, 0),
+        "x": halves_of(0, 3) + [(0, 1, 0)],
+        "y": halves_of(0, 0) + [(0, 1, 1), (1, 0, 0)],
         "up": halves_of(-1, 2) + halves_of(-1, 3),
-        "down": halves_of(1, 2) + halves_of(1, 1),
+        "down": halves_of(1, 2) + [(1, 0, 1)] + halves_of(1, 1),
     },
     {
         "x": halves_of(0, 2) + [(0, 0, 0), (1, 2, 0)],
@@ -398,14 +398,9 @@
         for at in range(PLANE):
             pl.when(place == at)(lambda: act(at))
 
-    def dispatch(kind):
-        def act(at):
-            for leaf in parts(kind):
-                on_links(kind, at, (0, at, leaf), start)
-
-        by_place(act)
-        for leaf in parts(kind):
-            relay(kind, 0, leaf).start()
+    def dispatch(kind, leaf):
+        by_place(lambda at: on_links(kind, at, (0, at, leaf), start))
+        relay(kind, 0, leaf).start()
 
     def serve(kind, step):
         def act(at):
@@ -451,29 +446,27 @@
     home = parent - low
     inputs[1].wait()
     pl.semaphore_wait(barrier, peers)
-    dispatch(0)
+    dispatch(0, 0)
     inputs[2].wait()
     reduce_blocks(diag_in, win_bases.at[here], bases_t, work, low_corner)
 
-    def between(panel_done):
-        if panel_done > 0 and panel_done < red // PANEL - 1:
-            serve(0, panel_done)
-
-    eliminate(win_shift.at[here], turned, work, rows, between)
-    dispatch(1)
-    blocks[...] = jnp.zeros_like(blocks)
-    halves[:, slots] = jnp.zeros_like(halves[:, slots])
+    def clear():
+        blocks[...] = jnp.zeros_like(blocks)
+        halves[:, slots] = jnp.zeros_like(halves[:, slots])
+
     reach = found.shape[1]
-    offset = lax.broadcasted_iota(jnp.int32, (reach, slots), 0) - reach // 2
-    order = lax.broadcasted_iota(jnp.int32, (reach, slots), 1)
-    inputs[0].wait()
-    for leaf in range(per_device):
-        away = offset + number + leaf
-        hit = (nbrs_in[leaf : leaf + 1, :] == away) & (away >= 0)
-        slot = jnp.max(jnp.where(hit, order, -1), axis=1, keepdims=True)
-        found[leaf] = jnp.broadcast_to(jnp.where(slot < 0, slots, slot), found.shape[1:])
     table = pltpu.make_async_copy(found, lookup, found_sem)
-    table.start()
+
+    def look_up():
+        offset = lax.broadcasted_iota(jnp.int32, (reach, slots), 0) - reach // 2
+        order = lax.broadcasted_iota(jnp.int32, (reach, slots), 1)
+        inputs[0].wait()
+        for leaf in range(per_device):
+            away = offset + number + leaf
+            hit = (nbrs_in[leaf : leaf + 1, :] == away) & (away >= 0)
+            slot = jnp.max(jnp.where(hit, order, -1), axis=1, keepdims=True)
+            found[leaf] = jnp.broadcast_to(jnp.where(slot < 0, slots, slot), found.shape[1:])
+        table.start()
 
     unroll = max(n for n in range(1, 14) if slots % n == 0)
 
@@ -578,40 +571,61 @@
             device_id_type=MESH,
         )
 
+    def send_rows():
+        for leaf in range(per_device):
+            column = pl.multiple_of(((number + leaf) % CHILDREN) * RANK, RANK)
+            blocks[leaf, home, :, pl.ds(column, RANK)] = skeleton[leaf]
+        for leaf in range(per_device):
+            diagonal[leaf] = blocks[leaf, home].astype(jnp.bfloat16)
+        for t in range(1, size):
+            row_copy(t).start()
+
+    def wait_near():
+        for copy in fetches:
+            copy.wait()
+        table.wait()
+
+    def between(panel_done):
+        pass
+        if panel_done == 0:
+            dispatch(0, 1)
+        if panel_done == 2:
+            serve(0, 1)
+
+    eliminate(win_shift.at[here], turned, work, rows, between)
+    dispatch(1, None)
+    finish_factor(factor, panel, skeleton, rows, low_corner)
+    clear()
+    look_up()
+    wait_near()
+    serve(0, 2)
+    project(0)
+    project(1)
+    run(first_half, 0)
+    run(first_half, 1)
+    serve(1, 1)
     serve(0, 3)
-    for copy in fetches:
-        copy.wait()
-    table.wait()
-    for turn in range(slots // unroll):
-        project(turn)
-    for turn in range(2):
-        run(first_half, turn)
-    serve(1, 1)
+    run(second_half, 0)
+    run(second_half, 1)
+    run(first_half, 2)
+    run(first_half, 3)
+    run(first_half, 4)
+    send_rows()
+    serve(1, 2)
+    run(second_half, 2)
+    run(second_half, 3)
+    run(second_half, 4)
     serve(0, 4)
-    for turn in range(2):
-        run(second_half, turn)
-    finish_factor(factor, panel, skeleton, rows, low_corner)
-    for leaf in range(per_device):
-        column = pl.multiple_of(((number + leaf) % CHILDREN) * RANK, RANK)
-        blocks[leaf, home, :, pl.ds(column, RANK)] = skeleton[leaf]
-    for leaf in range(per_device):
-        diagonal[leaf] = blocks[leaf, home].astype(jnp.bfloat16)
-    for t in range(1, size):
-        row_copy(t).start()
-    for turn in range(2, 5):
-        run(first_half, turn)
-    serve(1, 2)
-    for turn in range(2, 5):
-        run(second_half, turn)
-    for step in range(5, STEPS[0] + 1):
-        serve(0, step)
-    for turn in range(5, chunks):
-        run(first_half, turn)
-    for step in range(3, STEPS[1] + 1):
-        serve(1, step)
-    for turn in range(5, chunks):
-        run(second_half, turn)
-
+    run(first_half, 5)
+    run(first_half, 6)
+    serve(1, 3)
+    run(second_half, 5)
+    run(second_half, 6)
+    serve(0, 5)
+    run(first_half, 7)
+    run(first_half, 8)
+    run(second_half, 7)
+    run(second_half, 8)
     finish(0)
     finish(1)
     for t in range(1, size):

time: 39 us -> 37.2 us (0.954)
  Pallas kernels: 38 us -> 36.2 us
    pallas_call x1, Pallas kernels: 34.5 us -> 32.7 us  [local(): pl.pallas_call(functools.partial(level_kernel, count, parents, targets),...]
where the time goes in v5:
time: 37.2 us; the launch traced here: 37 us
  Pallas kernels  36.2 us (97%)
  between operations  0.82 us (2%)
    pallas_call x1, Pallas kernels, local(): pl.pallas_call(functools.partial(level_kernel, count, parents, targets),...  32.7 us
    pallas_call x1, Pallas kernels, local(): pl.pallas_call(place_kernel, out_shape=(out((per_device, red, red), f32),...  3.49 us

profile of v5, /device:TPU:17, one launch (start us, length us, event | category | flops | bytes accessed | tf_op | source)
XLA Modules:
  0.0 37.0 jit_solution(17657562596906716653)
XLA Ops:
  0.6 0.0 copy-start
  0.6 32.7 %level.1 = (f32[2,128,128]{2,1,0:T(8,128)S(1)}, f32[2,128,128]{2,1,0:T(8,128)S(1)}, f32[2,5,128,1024]{3,2,1,0:T(8,128)S(1)}, bf16[4,2,128,256]{3,2,1,0:T(8,128)(2,1)S(1)}) custom-call(s32[2,26]{1,0:T(2,128)} %nbrs.1, bf16[2,256,256]{2,1,0:T(8,128)(2,1)} %diag.1, bf16[2,256,256]{2,1,0:T(8,128)(2,1)} %bases.1, bf16[2,26,256,256]{3,2,1,0:T(8,128)(2,1)} %near.1), custom_call_target="tpu_custom_call" | custom-call | tf_op jit(solution)/shard_map/level/pallas_call | solution.py:696
  33.3 0.0 copy-done
  33.4 3.5 %place.1 = (f32[2,128,128]{2,1,0:T(8,128)}, f32[2,128,128]{2,1,0:T(8,128)}, f32[2,5,128,1024]{3,2,1,0:T(8,128)}, f32[256,1024]{1,0:T(8,128)}) custom-call(s32[8,5]{1,0:T(8,128)S(1)} %copy-done, f32[2,128,128]{2,1,0:T(8,128)S(1)} %get-tuple-element.8.factor, f32[2,128,128]{2,1,0:T(8,128)S(1)} %get-tuple-element.9.panel, ...), custom_call_target="tpu_custom_call" | custom-call | tf_op jit(solution)/shard_map/place/pallas_call | solution.py:739
Async XLA Ops:
  0.6 32.7 %copy-start = (s32[8,5]{1,0:T(8,128)S(1)}, s32[8,5]{1,0:T(8,128)}, u32[]{:S(2)}) copy-start(s32[8,5]{1,0:T(8,128)} %parents.1) | copy-start | bytes 484

commit v6 on v5

--- a/solution.py
+++ b/solution.py
@@ -37,7 +37,7 @@
     return [(plane, chip, None)]
 
 
-BASES_IN = (
+OUTER_IN = (
     {
         "x": halves_of(0, 1) + [(0, 3, 0), (-1, 1, 0)],
         "y": halves_of(0, 2) + [(0, 3, 1)] + halves_of(-1, 2),
@@ -63,7 +63,7 @@
         "down": halves_of(1, 3) + [(1, 2, 1)] + halves_of(1, 0),
     },
 )
-SHIFTS_IN = (
+LIFTED_IN = (
     {
         "x": whole(0, 1) + whole(-1, 1),
         "y": whole(0, 2) + whole(0, 3) + whole(-1, 2),
@@ -117,7 +117,7 @@
     return outbound, arrivals, now
 
 
-OUTBOUND, ARRIVALS, STEPS = zip(plan(BASES_IN), plan(SHIFTS_IN))
+OUTBOUND, ARRIVALS, STEPS = zip(plan(OUTER_IN), plan(LIFTED_IN))
 
 
 def shift_of(place, item):
@@ -154,7 +154,7 @@
         low_corner[leaf] = dense[red:, red:]
 
 
-def eliminate(shift, turned, work, rows, serve):
+def eliminate(bases, lifted, turned, work, rows, serve):
     per_device, red = work.shape[0], work.shape[1]
     tiles = work.shape[2] // LANES
     row_id = lax.broadcasted_iota(jnp.int32, (red, red), 0)
@@ -215,9 +215,9 @@
     for leaf in range(per_device):
         solved = rows[leaf, :, red : red + RANK]
         inverse = jnp.where(col_id <= row_id, rows[leaf, :, red + RANK :], 0.0)
-        moved = matmul_t(inverse, solved, highest)
-        shift[leaf] = moved.astype(jnp.bfloat16)
-        back = -moved.astype(jnp.bfloat16).astype(jnp.float32).T
+        shift = matmul_t(inverse, solved, highest).astype(jnp.bfloat16)
+        lifted[leaf] = matmul(bases[leaf, :, :red], shift).astype(jnp.bfloat16)
+        back = -shift.astype(jnp.float32).T
         turned[leaf, :, :red] = back.astype(jnp.bfloat16)
         turned[leaf, :, red:] = back.astype(jnp.bfloat16)
 
@@ -251,8 +251,9 @@
     panel,
     blocks,
     landed,
-    win_bases,
-    win_shift,
+    win_outer,
+    win_lifted,
+    bases_in,
     diag_in,
     nbrs_in,
     low_corner,
@@ -263,7 +264,6 @@
     rows,
     near_in,
     halves,
-    lefts,
     diagonal,
     send,
     recv,
@@ -300,7 +300,12 @@
     inputs = [
         pltpu.make_async_copy(source, target, in_sem.at[n])
         for n, (source, target) in enumerate(
-            ((nbrs, nbrs_in), (bases, win_bases.at[here]), (diag, diag_in))
+            (
+                (nbrs, nbrs_in),
+                (bases.at[:, :, pl.ds(red, RANK)], win_outer.at[here]),
+                (bases, bases_in),
+                (diag, diag_in),
+            )
         )
     ]
     for copy in inputs + fetches:
@@ -318,7 +323,7 @@
 
         peers = peers + present[link].astype(jnp.int32)
 
-    windows = (win_bases, win_shift)
+    windows = (win_outer, win_lifted)
 
     def exists(delta):
         return (chip + delta >= 0) & (chip + delta < total)
@@ -447,11 +452,17 @@
     inputs[1].wait()
     pl.semaphore_wait(barrier, peers)
     dispatch(0, 0)
-    inputs[2].wait()
-    reduce_blocks(diag_in, win_bases.at[here], bases_t, work, low_corner)
+    for copy in inputs[2:]:
+        copy.wait()
+    reduce_blocks(diag_in, bases_in, bases_t, work, low_corner)
 
     def clear():
-        blocks[...] = jnp.zeros_like(blocks)
+        for row in range(targets):
+
+            @pl.when((low + row < parent - 1) | (low + row > parent + 1))
+            def _(row=row):
+                blocks[:, row] = jnp.zeros_like(blocks[:, row])
+
         halves[:, slots] = jnp.zeros_like(halves[:, slots])
 
     reach = found.shape[1]
@@ -503,25 +514,21 @@
             else:
                 act(row, column, mine)
 
+    def slot_for(other, mine):
+        return lookup[mine, other - number - mine + reach // 2, 0]
+
     def first_half(turn):
         for leaf in parts(0):
             relayed(0, deltas[turn], leaf).wait_recv()
         coupled = {}
         targets_of = {}
         for holder, leaf, slot, other, row, column in pairs_of(turn):
-            left = []
+            left = [halves[mine, slot_for(other, mine)] for mine in range(per_device)]
+            both = matmul(jnp.concatenate(left, axis=0), win_outer[slot, leaf])
             for mine in range(per_device):
-                n = lookup[mine, other - number - mine + reach // 2, 0]
-                left.append(halves[mine, n])
                 targets_of[holder, leaf, mine] = (other, row, column, mine)
-            both = matmul(jnp.concatenate(left, axis=0), win_bases[slot, leaf])
-            for mine in range(per_device):
                 part = both[mine * 2 * RANK : (mine + 1) * 2 * RANK]
-                high, low_part = split(part[red:, :red])
-                here_rows = pl.ds(mine * RANK, RANK)
-                lefts[turn, holder, leaf, here_rows, :red] = high
-                lefts[turn, holder, leaf, here_rows, red:] = low_part
-                coupled[holder, leaf, mine] = (split(part[:red, red:]), part[red:, red:])
+                coupled[holder, leaf, mine] = (split(part[:red]), part[red:])
         kept = []
         for holder in range(2):
             for mine in range(per_device):
@@ -544,8 +551,8 @@
             relayed(1, deltas[turn], leaf).wait_recv()
         kept = []
         for holder, leaf, slot, other, row, column in pairs_of(turn):
-            moved = win_shift[slot, leaf]
-            both = matmul(lefts[turn, holder, leaf], jnp.concatenate([moved, moved], axis=0))
+            left = [halves[mine, slot_for(other, mine), red:] for mine in range(per_device)]
+            both = matmul(jnp.concatenate(left, axis=0), win_lifted[slot, leaf])
             for mine in range(per_device):
                 value = both[mine * RANK : (mine + 1) * RANK]
 
@@ -592,7 +599,7 @@
         if panel_done == 2:
             serve(0, 1)
 
-    eliminate(win_shift.at[here], turned, work, rows, between)
+    eliminate(bases_in, win_lifted.at[here], turned, work, rows, between)
     dispatch(1, None)
     finish_factor(factor, panel, skeleton, rows, low_corner)
     clear()
@@ -611,19 +618,19 @@
     run(first_half, 3)
     run(first_half, 4)
     send_rows()
+    serve(0, 4)
     serve(1, 2)
     run(second_half, 2)
     run(second_half, 3)
     run(second_half, 4)
-    serve(0, 4)
     run(first_half, 5)
     run(first_half, 6)
+    serve(0, 5)
+    run(first_half, 7)
+    run(first_half, 8)
     serve(1, 3)
     run(second_half, 5)
     run(second_half, 6)
-    serve(0, 5)
-    run(first_half, 7)
-    run(first_half, 8)
     run(second_half, 7)
     run(second_half, 8)
     finish(0)
@@ -704,8 +711,9 @@
         in_specs=[hbm] * 4,
         out_specs=(vmem,) * 4,
         scratch_shapes=[
-            pltpu.VMEM((window,) + bases.shape, bf16),
-            pltpu.VMEM((window, per_device, red, RANK), bf16),
+            pltpu.VMEM((window, per_device, leaf_rows, RANK), bf16),
+            pltpu.VMEM((window, per_device, leaf_rows, RANK), bf16),
+            pltpu.VMEM(bases.shape, bf16),
             pltpu.VMEM(diag_blocks.shape, bf16),
             pltpu.VMEM(leaf_nbrs.shape, jnp.int32),
             pltpu.VMEM((per_device, RANK, RANK), f32),
@@ -716,13 +724,12 @@
             pltpu.VMEM((per_device, red, 2 * red + RANK), f32),
             pltpu.VMEM(near_blocks.shape, bf16),
             pltpu.VMEM((per_device, slots + 1) + near_blocks.shape[2:], bf16),
-            pltpu.VMEM((2 * PLANE + 1, 2, per_device, per_device * RANK, 2 * red), bf16),
             pltpu.VMEM((per_device, RANK, CHILDREN * RANK), bf16),
             sems((2, len(LINKS), links)),
             sems((2, 2 * PLANE + 1, per_device)),
             sems((2, 2 * PLANE + 1, per_device)),
             sems((2, 2 * PLANE + 1, per_device)),
-            sems((3,)),
+            sems((4,)),
             sems((per_device,)),
             sems((size,)),
             sems((size,)),

time: 37.2 us -> 34.6 us (0.930)
  Pallas kernels: 36.2 us -> 33.5 us
    pallas_call x1, Pallas kernels: 32.7 us -> 30 us  [local(): pl.pallas_call(functools.partial(level_kernel, count, parents, targets),...]
where the time goes in v6:
time: 34.6 us; the launch traced here: 34.3 us
  Pallas kernels  33.5 us (97%)
  between operations  0.82 us (2%)
    pallas_call x1, Pallas kernels, local(): pl.pallas_call(functools.partial(level_kernel, count, parents, targets),...  30 us
    pallas_call x1, Pallas kernels, local(): pl.pallas_call(place_kernel, out_shape=(out((per_device, red, red), f32),...  3.49 us

profile of v6, /device:TPU:17, one launch (start us, length us, event | category | flops | bytes accessed | tf_op | source)
XLA Modules:
  0.0 34.3 jit_solution(15705495399426438157)
XLA Ops:
  0.6 0.0 copy-start
  0.6 30.0 %level.1 = (f32[2,128,128]{2,1,0:T(8,128)S(1)}, f32[2,128,128]{2,1,0:T(8,128)S(1)}, f32[2,5,128,1024]{3,2,1,0:T(8,128)S(1)}, bf16[4,2,128,256]{3,2,1,0:T(8,128)(2,1)S(1)}) custom-call(s32[2,26]{1,0:T(2,128)} %nbrs.1, bf16[2,256,256]{2,1,0:T(8,128)(2,1)} %diag.1, bf16[2,256,256]{2,1,0:T(8,128)(2,1)} %bases.1, bf16[2,26,256,256]{3,2,1,0:T(8,128)(2,1)} %near.1), custom_call_target="tpu_custom_call" | custom-call | tf_op jit(solution)/shard_map/level/pallas_call | solution.py:703
  30.6 0.0 copy-done
  30.6 3.5 %place.1 = (f32[2,128,128]{2,1,0:T(8,128)}, f32[2,128,128]{2,1,0:T(8,128)}, f32[2,5,128,1024]{3,2,1,0:T(8,128)}, f32[256,1024]{1,0:T(8,128)}) custom-call(s32[8,5]{1,0:T(8,128)S(1)} %copy-done, f32[2,128,128]{2,1,0:T(8,128)S(1)} %get-tuple-element.8.factor, f32[2,128,128]{2,1,0:T(8,128)S(1)} %get-tuple-element.9.panel, ...), custom_call_target="tpu_custom_call" | custom-call | tf_op jit(solution)/shard_map/place/pallas_call | solution.py:746
Async XLA Ops:
  0.6 30.0 %copy-start = (s32[8,5]{1,0:T(8,128)S(1)}, s32[8,5]{1,0:T(8,128)}, u32[]{:S(2)}) copy-start(s32[8,5]{1,0:T(8,128)} %parents.1) | copy-start | bytes 484

commit v7 on v6

--- a/solution.py
+++ b/solution.py
@@ -114,6 +114,8 @@
         for target, item in landed:
             held[target][item] = now
             arrivals[target].append((now, item))
+    for events in arrivals:
+        events.sort(key=lambda event: (event[0], event[1][0] != 0))
     return outbound, arrivals, now
 
 

time: 34.6 us -> 32.3 us (0.934)
  Pallas kernels: 33.5 us -> 31.2 us
    pallas_call x1, Pallas kernels: 30 us -> 27.7 us  [local(): pl.pallas_call(functools.partial(level_kernel, count, parents, targets),...]
where the time goes in v7:
time: 32.3 us; the launch traced here: 32 us
  Pallas kernels  31.2 us (97%)
  between operations  0.82 us (3%)
    pallas_call x1, Pallas kernels, local(): pl.pallas_call(functools.partial(level_kernel, count, parents, targets),...  27.7 us
    pallas_call x1, Pallas kernels, local(): pl.pallas_call(place_kernel, out_shape=(out((per_device, red, red), f32),...  3.49 us

profile of v7, /device:TPU:17, one launch (start us, length us, event | category | flops | bytes accessed | tf_op | source)
XLA Modules:
  0.0 32.0 jit_solution(10216958194304906156)
XLA Ops:
  0.6 0.0 copy-start
  0.6 27.7 %level.1 = (f32[2,128,128]{2,1,0:T(8,128)S(1)}, f32[2,128,128]{2,1,0:T(8,128)S(1)}, f32[2,5,128,1024]{3,2,1,0:T(8,128)S(1)}, bf16[4,2,128,256]{3,2,1,0:T(8,128)(2,1)S(1)}) custom-call(s32[2,26]{1,0:T(2,128)} %nbrs.1, bf16[2,256,256]{2,1,0:T(8,128)(2,1)} %diag.1, bf16[2,256,256]{2,1,0:T(8,128)(2,1)} %bases.1, bf16[2,26,256,256]{3,2,1,0:T(8,128)(2,1)} %near.1), custom_call_target="tpu_custom_call" | custom-call | tf_op jit(solution)/shard_map/level/pallas_call | solution.py:705
  28.3 0.0 copy-done
  28.3 3.5 %place.1 = (f32[2,128,128]{2,1,0:T(8,128)}, f32[2,128,128]{2,1,0:T(8,128)}, f32[2,5,128,1024]{3,2,1,0:T(8,128)}, f32[256,1024]{1,0:T(8,128)}) custom-call(s32[8,5]{1,0:T(8,128)S(1)} %copy-done, f32[2,128,128]{2,1,0:T(8,128)S(1)} %get-tuple-element.8.factor, f32[2,128,128]{2,1,0:T(8,128)S(1)} %get-tuple-element.9.panel, ...), custom_call_target="tpu_custom_call" | custom-call | tf_op jit(solution)/shard_map/place/pallas_call | solution.py:748
Async XLA Ops:
  0.6 27.7 %copy-start = (s32[8,5]{1,0:T(8,128)S(1)}, s32[8,5]{1,0:T(8,128)}, u32[]{:S(2)}) copy-start(s32[8,5]{1,0:T(8,128)} %parents.1) | copy-start | bytes 484
